TPU v7x, 32 devices: a whole 2x2x4 slice. The times are simulated.
32 devices in a mesh: dp: 8 (over z, x), mp: 4 (over y, core).
Axes of the slice: x: 2, y: 2, z: 4, core: 2. Of those that a mesh axis runs over, the one named last changes fastest.
Arguments:
- hash_codes: int32 [8192, 2048], P('dp'), may hold values from 0 to 32703, as said below
- w_hash: bfloat16 [2048, 8192], P(None, 'mp'), may hold values from -0.125 to 0.125
- norm_gain: float32 [8192], P('mp'), may hold values from 0.1 to 1.9
- norm_bias: float32 [8192], P('mp'), may hold values from -3 to 3
- w_out: bfloat16 [8192, 256], P('mp'), may hold values from -0.0625 to 0.0625
- dense_vectors: bfloat16 [8192, 8, 256], P('dp'), may hold values from -6 to 6
- field_mix: float32 [8], replicated, may hold values from -3 to 3
- labels: int32 [8192], P('dp'), may hold values 0 or 1
Outputs:
- grad_hash: float32 [2048, 8192], P('dp', 'mp')
- grad_gain: float32 [8192], P('mp')
- grad_bias: float32 [8192], P('mp')
- grad_out: float32 [8192, 256], P('mp')
- mean_loss: float32 [], replicated
Inputs may be any that keep to these rules, and one draw needn't show every extreme that they name: `hash_codes`: codes of fixed universal hashes of each id.
All inputs are finite; a program needn't handle non-finite values. No bound on the sum of `labels` on one device may be relied on, other than what follows from the above.
Results may differ from a plain program's by a relative error of at most 0.011.
Values may be sent and summed in bfloat16 or wider, within the bound.
A program may use at most 192 MiB of HBM per device.

v0:
```python
import math

import jax
import jax.numpy as jnp
from jax import lax
from jax.sharding import PartitionSpec as P

EMB = 256


buckets = 32704.0
epsilon = 1e-05
grad_scale = 32.0


def mish_parts(pre_act):
    softer = jax.nn.softplus(pre_act)
    tangent = jnp.tanh(softer)
    value = pre_act * tangent
    mish_slope = tangent + pre_act * jax.nn.sigmoid(pre_act) * (1.0 - tangent * tangent)
    return (value, mish_slope)


def interact(embedding, dense_vectors, field_mix, labels, total_rows):
    scores = jnp.sum(embedding[:, None, :] * dense_vectors, -1)
    logits = jnp.sum(scores * field_mix, -1) / math.sqrt(EMB)
    targets = labels.astype(jnp.float32)
    loss_local = jnp.sum(jax.nn.softplus(logits) - targets * logits)
    grad_logits = (jax.nn.sigmoid(logits) - targets) * (grad_scale / math.sqrt(total_rows))
    grad_scores = grad_logits[:, None] * field_mix / math.sqrt(EMB)
    grad_embed = jnp.sum(grad_scores[:, :, None] * dense_vectors, 1).astype(jnp.bfloat16)
    return (grad_embed, loss_local)


def on_device(hash_codes, w_hash, norm_gain, norm_bias, w_out, dense_vectors, field_mix, labels):
    row_count = hash_codes.shape[0]
    dp_count = lax.axis_size("dp")
    mp_count = lax.axis_size("mp")
    total_rows = row_count * dp_count
    inputs = (hash_codes.astype(jnp.float32) * (2.0 / (buckets - 1.0)) - 1.0).astype(jnp.bfloat16)
    pre_act = jnp.dot(inputs, w_hash, preferred_element_type=jnp.float32)
    hidden, mish_slope = mish_parts(pre_act)
    sum_first, sum_second = lax.psum((jnp.sum(hidden, 0), jnp.sum(hidden * hidden, 0)), "dp")
    unit_mean = sum_first / total_rows
    unit_var = sum_second / total_rows - unit_mean * unit_mean
    inv_std = lax.rsqrt(unit_var + epsilon)
    centred = (hidden - unit_mean) * inv_std
    normed = (norm_gain * centred + norm_bias).astype(jnp.bfloat16)
    row_share = row_count // mp_count
    embedding = lax.psum_scatter(
        jnp.dot(normed, w_out, preferred_element_type=jnp.float32),
        "mp",
        scatter_dimension=0,
        tiled=True,
    )
    row_begin = lax.axis_index("mp") * row_share
    dense_part = lax.dynamic_slice_in_dim(dense_vectors, row_begin, row_share, 0)
    label_part = lax.dynamic_slice_in_dim(labels, row_begin, row_share, 0)
    embed_part, loss_local = interact(embedding, dense_part, field_mix, label_part, total_rows)
    grad_embed = lax.all_gather(embed_part, "mp", axis=0, tiled=True)
    loss_part = lax.psum(loss_local, "mp")
    out_local = lax.dot_general(
        normed, grad_embed, (((0,), (0,)), ((), ())), preferred_element_type=jnp.float32
    )
    grad_out, loss_total = lax.psum((out_local, loss_part), "dp")
    mean_loss = loss_total / total_rows
    grad_normed = lax.dot_general(
        grad_embed, w_out, (((1,), (1,)), ((), ())), preferred_element_type=jnp.float32
    )
    grad_bias, grad_gain = lax.psum(
        (jnp.sum(grad_normed, 0), jnp.sum(grad_normed * centred, 0)), "dp"
    )
    grad_hidden = inv_std * (
        norm_gain * grad_normed
        - norm_gain * grad_bias / total_rows
        - centred * norm_gain * grad_gain / total_rows
    )
    grad_pre = (grad_hidden * mish_slope).astype(jnp.bfloat16)
    grad_hash = lax.psum_scatter(
        lax.dot_general(
            inputs, grad_pre, (((0,), (0,)), ((), ())), preferred_element_type=jnp.float32
        ),
        "dp",
        scatter_dimension=0,
        tiled=True,
    )
    return (grad_hash, grad_gain, grad_bias, grad_out, mean_loss)


def solution(mesh):
    in_specs = (
        P("dp", None),
        P(None, "mp"),
        P("mp"),
        P("mp"),
        P("mp", None),
        P("dp", None, None),
        P(),
        P("dp"),
    )
    out_specs = (P("dp", "mp"), P("mp"), P("mp"), P("mp", None), P())
    return jax.shard_map(
        on_device, mesh=mesh, in_specs=in_specs, out_specs=out_specs, check_vma=False
    )
```

profile of v0, /device:TPU:10, one launch (start us, length us, event | category | flops | bytes accessed | tf_op | source)
XLA Modules:
  0.0 565.1 jit_solution(8014096853422411796)
XLA Ops:
  7.2 0.0 copy-start
  7.2 0.0 copy-start.4
  7.2 0.0 copy-start.1
  7.2 0.0 reduce-scatter.3.cloned.1.call-start
  7.2 20.5 %multiply_reduce_fusion.1 = (f32[2048]{0:T(1024)S(1)}, f32[2048]{0:T(1024)S(1)}, f32[1024,2048]{1,0:T(8,128)}) fusion(bf16[2048,2048]{1,0:T(8,128)(2,1)} %param.9, s32[1024,2048]{1,0:T(8,128)} %param.8), kind=kOutput, calls=%fused_computation.6 | convolution fusion | flops 8619290624 | bytes 25182208 | tf_op jit(solution)/shard_map/dot_general | solution.py:41
  27.7 30.1 %all-reduce.1 = (f32[2048]{0:T(1024)S(1)}, f32[2048]{0:T(1024)S(1)}) all-reduce(f32[2048]{0:T(1024)S(1)} %get-tuple-element.8, f32[2048]{0:T(1024)S(1)} %get-tuple-element.7), channel_id=1, replica_groups=mesh['dp'=8,'mp'=4] {'dp'}, use_global_device_ids=true, to_apply=%region_3.4 | all-reduce | flops 4096 | bytes 32768 | tf_op jit(solution)/shard_map/psum | solution.py:43
  57.8 0.0 copy-done
  57.8 0.0 copy-done.4
  57.8 0.0 copy-done.1
  57.9 0.0 copy-start.3
  57.9 9.7 %fusion.7 = f32[1024,256]{1,0:T(8,128)} fusion(bf16[2048,256]{1,0:T(8,128)(2,1)S(1)} %copy-done, f32[2048]{0:T(1024)S(1)} %copy-done.4, f32[2048]{0:T(1024)S(1)} %get-tuple-element.15, f32[2048]{0:T(1024)S(1)} %copy-done.1, f32[2048]{0:T(1024)S(1)} %get-tuple-element.14, f32[1024,2048]{1,0:T(8,128)} %get-tuple-element.18), kind=kOutput, calls=%fused_computation.18 | convolution fusion | flops 1098907648 | bytes 10518528 | tf_op jit(solution)/shard_map/dot_general | solution.py:51
  67.5 0.0 reduce-scatter.3.cloned.1.call-update
  67.6 0.0 all-reduce.4.cloned.1.call-start
  67.6 29.3 %reduce-scatter.3.cloned.1.call-done = f32[256,256]{1,0:T(8,128)} async-done(((f32[1024,256]{1,0:T(8,128)}), f32[256,256]{1,0:T(8,128)}) %reduce-scatter.3.cloned.1.call-update) | async-done | bytes 262160 | tf_op jit(solution)/shard_map/reduce_scatter | solution.py:50
  96.9 1.7 fusion.3
  98.6 0.0 copy-done.3
  98.6 0.1 multiply_reduce_fusion.2
  98.7 1.4 fusion.9
  100.1 0.1 multiply_multiply_fusion
  100.2 0.0 slice-start
  100.2 2.1 fusion.4
  102.3 6.8 %all_gather.3 = bf16[1024,256]{1,0:T(8,128)(2,1)S(1)} all-gather(bf16[256,256]{1,0:T(8,128)(2,1)S(1)} %fusion.4), channel_id=1, replica_groups=mesh['dp'=8,'mp'=4] {'mp'}, dimensions={0}, use_global_device_ids=true | all-gather | bytes 655360 | tf_op jit(solution)/shard_map/all_gather | solution.py:60
  109.1 0.0 slice-start.1
  109.1 10.9 %fusion.22 = (f32[2048]{0:T(1024)S(1)}, f32[2048]{0:T(1024)S(1)}, f32[1024,2048]{1,0:T(8,128)}) fusion(f32[2048]{0:T(1024)S(1)} %get-tuple-element.14, f32[2048]{0:T(1024)S(1)} %get-tuple-element.15, f32[1024,2048]{1,0:T(8,128)} %get-tuple-element.18, bf16[1024,256]{1,0:T(8,128)(2,1)S(1)} %all_gather.3, bf16[2048,256]{1,0:T(8,128)(2,1)S(1)} %copy-done), kind=kOutput, calls=%fused_computation.35 | convolution fusion | flops 1098903552 | bytes 18382848 | tf_op jit(solution)/shard_map/dot_general | solution.py:67
  120.0 0.0 slice-done
  120.0 0.0 slice-done.1
  120.0 7.5 %fusion.6 = f32[2048,256]{1,0:T(8,128)} fusion(bf16[1024,256]{1,0:T(8,128)(2,1)S(1)} %all_gather.3, f32[2048]{0:T(1024)S(1)} %copy-done.4, f32[2048]{0:T(1024)S(1)} %get-tuple-element.15, f32[2048]{0:T(1024)S(1)} %copy-done.1, f32[2048]{0:T(1024)S(1)} %get-tuple-element.14, f32[1024,2048]{1,0:T(8,128)S(1)} %bitcast.6), kind=kOutput, calls=%fused_computation.17 | convolution fusion | flops 1098907648 | bytes 11042816 | tf_op jit(solution)/shard_map/dot_general | solution.py:62
  127.6 7.3 %psum.54 = f32[]{:T(128)} all-reduce(f32[]{:T(128)} %get-tuple-element.16), channel_id=1, replica_groups=mesh['dp'=8,'mp'=4] {'mp'}, use_global_device_ids=true, to_apply=%region_15.16 | all-reduce | flops 1 | bytes 8 | tf_op jit(solution)/shard_map/psum | solution.py:61
  134.9 30.6 %all-reduce = (f32[2048]{0:T(1024)S(1)}, f32[2048]{0:T(1024)S(1)}, f32[]{:T(128)}) all-reduce(f32[2048]{0:T(1024)S(1)} %get-tuple-element.6, f32[2048]{0:T(1024)S(1)} %get-tuple-element.5, f32[]{:T(128)} %psum.54), channel_id=1, replica_groups=mesh['dp'=8,'mp'=4] {'dp'}, use_global_device_ids=true, to_apply=%region_11.12 | all-reduce | flops 4097 | bytes 32776 | tf_op jit(solution)/shard_map/psum | solution.py:70
  165.5 0.0 copy-start.2
  165.5 0.0 copy-start.5
  165.5 0.0 all-reduce.4.cloned.1.call-update
  165.5 0.3 reduce-scatter.5.cloned.1.call-start
  165.8 27.8 %fusion.2 = f32[2048,2048]{1,0:T(8,128)} fusion(f32[1024,2048]{1,0:T(8,128)} %get-tuple-element.18, f32[1024,2048]{1,0:T(8,128)} %get-tuple-element.19, f32[2048]{0:T(1024)S(1)} %get-tuple-element.21, f32[2048]{0:T(1024)S(1)} %multiply_multiply_fusion.1, f32[2048]{0:T(1024)S(1)} %get-tuple-element.15, f32[2048]{0:T(1024)S(1)} %copy-done.1, ...), kind=kOutput, calls=%fused_computation.9 | convolution fusion | flops 8652849152 | bytes 41984000 | tf_op jit(solution)/shard_map/dot_general | solution.py:80
  193.6 0.0 copy-done.2
  193.6 0.0 copy-done.5
  193.6 0.0 reduce-scatter.5.cloned.1.call-update
  194.3 77.6 %all-reduce.4.cloned.1.call-done = f32[2048,256]{1,0:T(8,128)} async-done(((f32[2048,256]{1,0:T(8,128)}), f32[2048,256]{1,0:T(8,128)}) %all-reduce.4.cloned.1.call-update) | async-done | bytes 2097168 | tf_op jit(solution)/shard_map/psum | solution.py:65
  271.9 282.5 %reduce-scatter.5.cloned.1.call-done = f32[256,2048]{1,0:T(8,128)} async-done(((f32[2048,2048]{1,0:T(8,128)}), f32[256,2048]{1,0:T(8,128)}) %reduce-scatter.5.cloned.1.call-update) | async-done | bytes 2097168 | tf_op jit(solution)/shard_map/reduce_scatter | solution.py:79
  554.4 3.0 copy.14
  (3 shorter events, 0.0 us)
Async XLA Ops:
  7.2 50.7 %copy-start = (bf16[2048,256]{1,0:T(8,128)(2,1)S(1)}, bf16[2048,256]{1,0:T(8,128)(2,1)}, u32[]{:S(2)}) copy-start(bf16[2048,256]{1,0:T(8,128)(2,1)} %param.12) | copy-start | bytes 3145732
  7.2 50.7 %copy-start.4 = (f32[2048]{0:T(1024)S(1)}, f32[2048]{0:T(1024)}, u32[]{:S(2)}) copy-start(f32[2048]{0:T(1024)} %param.11) | copy-start | bytes 24580
  7.2 50.7 %copy-start.1 = (f32[2048]{0:T(1024)S(1)}, f32[2048]{0:T(1024)}, u32[]{:S(2)}) copy-start(f32[2048]{0:T(1024)} %param.10) | copy-start | bytes 24580
  7.2 89.7 %reduce-scatter.3.cloned.1.call-start = ((), (), s32[]{:S(2)}) async-start(), calls=%async_computation.2 | async-start | bytes 1310720 | tf_op jit(solution)/shard_map/reduce_scatter | solution.py:50
  57.9 40.7 %copy-start.3 = (f32[8]{0:T(128)S(1)}, f32[8]{0:T(128)}, u32[]{:S(2)}) copy-start(f32[8]{0:T(128)} %param.14) | copy-start | bytes 100
  67.6 204.3 %all-reduce.4.cloned.1.call-start = ((), (), s32[]{:S(2)}) async-start(), calls=%async_computation.4 | async-start | bytes 4194304 | tf_op jit(solution)/shard_map/psum | solution.py:65
  100.2 19.8 %slice-start = ((s8[8388608]{0:T(1024)(128)(4,1)}), s8[4194304]{0:T(1024)(128)(4,1)S(1)}, s32[]{:S(2)}) async-start(s8[8388608]{0:T(1024)(128)(4,1)} %bitcast.5), calls=%async_computation.5 | async-start | bytes 8388608
  109.1 10.9 %slice-start.1 = ((s8[8388608]{0:T(1024)(128)(4,1)}), s8[4194304]{0:T(1024)(128)(4,1)S(1)}, s32[]{:S(2)}) async-start(s8[8388608]{0:T(1024)(128)(4,1)} %bitcast.5), calls=%async_computation.6 | async-start | bytes 8388608
  165.5 28.1 %copy-start.2 = (f32[2048]{0:T(1024)}, f32[2048]{0:T(1024)S(1)}, u32[]{:S(2)}) copy-start(f32[2048]{0:T(1024)S(1)} %get-tuple-element.22) | copy-start | bytes 24580
  165.5 28.1 %copy-start.5 = (f32[2048]{0:T(1024)}, f32[2048]{0:T(1024)S(1)}, u32[]{:S(2)}) copy-start(f32[2048]{0:T(1024)S(1)} %get-tuple-element.21) | copy-start | bytes 24580
  165.5 388.9 %reduce-scatter.5.cloned.1.call-start = ((), (), s32[]{:S(2)}) async-start(), calls=%async_computation.3 | async-start | bytes 18874368 | tf_op jit(solution)/shard_map/reduce_scatter | solution.py:79
Sparse Core Ops, SparseCore 0:
  67.7 29.2 reduce-scatter.2
  165.6 106.1 all-reduce.3
  276.2 278.0 reduce-scatter.4
where the time goes:
time: 568 us; the launch traced here: 565 us
  waiting for transfers between devices  389 us (68%)
  matrix products  76.4 us (13%)
  blocking collectives  74.8 us (13%)
  between operations  15.6 us (3%)
    reduce_scatter x1, waiting for transfers between devices, on_device(): lax.psum_scatter(lax.dot_general(inputs, grad_pre, (((0,), (0,)), ((), ()...  283 us
    psum x1, waiting for transfers between devices, on_device(): grad_out, loss_total = lax.psum((out_local, loss_part), 'dp')  77.6 us
    psum x1, blocking collectives, on_device(): lax.psum((jnp.sum(grad_normed, 0), jnp.sum(grad_normed * centred, 0)), 'dp')  30.6 us
    psum x1, blocking collectives, on_device(): lax.psum((jnp.sum(hidden, 0), jnp.sum(hidden * hidden, 0)), 'dp')  30.1 us
    reduce_scatter x1, waiting for transfers between devices, on_device(): lax.psum_scatter(jnp.dot(normed, w_out, preferred_element_type=jnp.float3...  29.3 us
    dot_general x1, matrix products, on_device(): lax.dot_general(inputs, grad_pre, (((0,), (0,)), ((), ())), preferred_ele...  27.8 us
    dot_general x1, matrix products, on_device(): pre_act = jnp.dot(inputs, w_hash, preferred_element_type=jnp.float32)  20.5 us
  transfers between devices with their start and end apart: 3, of which 3 were waited for; matrix products, arithmetic and copies ran while one was open for 5% of the time, Pallas kernels for 0%

commit v1 on v0

v1 whole, which is shorter than its diff:
```python
import functools
import math

import jax
import jax.numpy as jnp
from jax import lax
from jax.experimental import pallas as pl
from jax.experimental.pallas import tpu as pltpu
from jax.sharding import PartitionSpec as P

EMB = 256
PAIR = 2
MESH = pl.DeviceIdType.MESH

buckets = 32704.0
epsilon = 1e-05
grad_scale = 32.0


def mish_parts(pre_act):
    grown = jnp.exp(jnp.minimum(pre_act, 20.0))
    numer = grown * (grown + 2.0)
    inverse = 1.0 / (numer + 2.0)
    tangent = numer * inverse
    value = pre_act * tangent
    mish_slope = tangent + pre_act * (4.0 * (grown * inverse) * ((1.0 + grown) * inverse))
    return (value, mish_slope)


def interact(embedding, dense_vectors, field_mix, labels, total_rows):
    scores = jnp.sum(embedding[:, None, :] * dense_vectors, -1)
    logits = jnp.sum(scores * field_mix, -1) / math.sqrt(EMB)
    targets = labels.astype(jnp.float32)
    loss_local = jnp.sum(jax.nn.softplus(logits) - targets * logits)
    grad_logits = (jax.nn.sigmoid(logits) - targets) * (grad_scale / math.sqrt(total_rows))
    grad_scores = grad_logits[:, None] * field_mix / math.sqrt(EMB)
    grad_embed = jnp.sum(grad_scores[:, :, None] * dense_vectors, 1).astype(jnp.bfloat16)
    return (grad_embed, loss_local)


def group_of(kind):
    dp, mp = lax.axis_index("dp"), lax.axis_index("mp")
    dp_n, mp_n = lax.axis_size("dp"), lax.axis_size("mp")
    if kind == "dp":
        return dp, dp_n, lambda place: (place, mp)
    if kind == "far":
        return dp // PAIR, dp_n // PAIR, lambda place: (place * PAIR + dp % PAIR, mp)
    here = (dp % PAIR) * mp_n + mp
    return here, PAIR * mp_n, lambda place: ((dp // PAIR) * PAIR + place // mp_n, place % mp_n)


def exchange_kernel(kinds, modes, *refs):
    count = len(kinds)
    sources, results = refs[:count], refs[count : 2 * count]
    sends, receives, locals_ = refs[2 * count : 3 * count], refs[3 * count : 4 * count], refs[4 * count]
    me, size, device = group_of(kinds[0])
    barrier = pltpu.get_barrier_semaphore()
    for step in range(1, size):
        pl.semaphore_signal(
            barrier, inc=1, device_id=device(lax.rem(me + step, size)), device_id_type=MESH
        )
    pl.semaphore_wait(barrier, size - 1)
    copies = []
    for at in range(count):
        me, size, device = group_of(kinds[at])
        for step in range(1, size):
            place = lax.rem(me + step, size)
            source = sources[at] if modes[at] == "gather" else sources[at].at[place]
            copy = pltpu.make_async_remote_copy(
                src_ref=source,
                dst_ref=results[at].at[me],
                send_sem=sends[at].at[step - 1],
                recv_sem=receives[at].at[step - 1],
                device_id=device(place),
                device_id_type=MESH,
            )
            copy.start()
            copies.append(copy)
        own = sources[at] if modes[at] == "gather" else sources[at].at[me]
        copy = pltpu.make_async_copy(own, results[at].at[me], locals_.at[at])
        copy.start()
        copies.append(copy)
    for copy in copies:
        copy.wait()


def exchange(operands, kinds, modes, ident, space=pltpu.VMEM):
    sizes = [group_of(kind)[1] for kind in kinds]
    shapes = []
    for operand, size, mode in zip(operands, sizes, modes):
        block = operand.shape if mode == "gather" else operand.shape[1:]
        shapes.append(jax.ShapeDtypeStruct((size,) + block, operand.dtype))
    semaphores = [pltpu.SemaphoreType.DMA((size - 1,)) for size in sizes]
    return pl.pallas_call(
        functools.partial(exchange_kernel, kinds, modes),
        out_shape=shapes,
        in_specs=[pl.BlockSpec(memory_space=space)] * len(operands),
        out_specs=[pl.BlockSpec(memory_space=space)] * len(operands),
        scratch_shapes=semaphores + semaphores + [pltpu.SemaphoreType.DMA((len(operands),))],
        compiler_params=pltpu.CompilerParams(collective_id=ident, has_side_effects=True),
    )(*operands)


def share_kernel(pieces, rows_ref, out_ref, near_send, near_recv, far_send, far_recv, core_send, core_recv):
    dp, mp, mp_n = lax.axis_index("dp"), lax.axis_index("mp"), lax.axis_size("mp")
    chips = mp_n // 2
    chip, core = mp // 2, mp % 2
    mate = (dp + 1 - 2 * (dp % PAIR), mp)
    other = (dp, mp + 1 - 2 * core)
    length = rows_ref.shape[0] // (mp_n * pieces)

    def across(step):
        return (dp, lax.rem(chip + step, chips) * 2 + core)

    def part(owner, piece):
        return pl.ds(pl.multiple_of((owner * pieces + piece) * length, length), length)

    def send(source, owner, piece, send_sem, recv_sem, target):
        copy = pltpu.make_async_remote_copy(
            src_ref=source.at[part(owner, piece)],
            dst_ref=out_ref.at[part(owner, piece)],
            send_sem=send_sem,
            recv_sem=recv_sem,
            device_id=target,
            device_id_type=MESH,
        )
        copy.start()
        return copy

    barrier = pltpu.get_barrier_semaphore()
    for target in [mate, other] + [across(step) for step in range(1, chips)]:
        pl.semaphore_signal(barrier, inc=1, device_id=target, device_id_type=MESH)
    pl.semaphore_wait(barrier, chips + 1)

    near = [
        send(rows_ref, mp, piece, near_send.at[piece], near_recv.at[piece], mate)
        for piece in range(pieces)
    ]
    far, cores = [], []
    for piece in range(pieces):
        near[piece].wait_recv()
        far.append(
            [
                send(out_ref, mp, piece, far_send.at[piece, step - 1], far_recv.at[piece, step - 1], across(step))
                for step in range(1, chips)
            ]
        )
        cores.append(send(out_ref, mp, piece, core_send.at[piece, 0], core_recv.at[piece, 0], other))
    for piece in range(pieces):
        for step in range(1, chips):
            far[piece][step - 1].wait_recv()
            owner = lax.rem(chip - step + chips, chips) * 2 + core
            cores.append(
                send(out_ref, owner, piece, core_send.at[piece, step], core_recv.at[piece, step], other)
            )
    for copy in cores:
        copy.wait()
    for piece in range(pieces):
        near[piece].wait_send()
        for copy in far[piece]:
            copy.wait_send()


def mate_rows(rows, ident):
    chips = lax.axis_size("mp") // 2
    pieces = 4
    dma = pltpu.SemaphoreType.DMA
    return pl.pallas_call(
        functools.partial(share_kernel, pieces),
        out_shape=jax.ShapeDtypeStruct(rows.shape, rows.dtype),
        in_specs=[pl.BlockSpec(memory_space=pl.ANY)],
        out_specs=pl.BlockSpec(memory_space=pl.ANY),
        scratch_shapes=[dma((pieces,)), dma((pieces,))]
        + [dma((pieces, max(chips - 1, 1)))] * 2
        + [dma((pieces, chips))] * 2,
        compiler_params=pltpu.CompilerParams(collective_id=ident, has_side_effects=True),
    )(rows)


def on_device(hash_codes, w_hash, norm_gain, norm_bias, w_out, dense_vectors, field_mix, labels):
    row_count = hash_codes.shape[0]
    dp_count = lax.axis_size("dp")
    mp_count = lax.axis_size("mp")
    far_count = dp_count // PAIR
    total_rows = row_count * dp_count
    codes, units = w_hash.shape
    half = units // PAIR
    side = lax.axis_index("dp") % PAIR
    f32, bf16 = jnp.float32, jnp.bfloat16

    def mine(array, axis):
        return lax.dynamic_slice_in_dim(array, side * half, half, axis)

    weights, gain, bias, out_rows = mine(w_hash, 1), mine(norm_gain, 0), mine(norm_bias, 0), mine(w_out, 0)
    inputs = (hash_codes.astype(f32) * (2.0 / (buckets - 1.0)) - 1.0).astype(bf16)
    mates = mate_rows(inputs, 0)

    acts = [mish_parts(jnp.dot(part, weights, preferred_element_type=f32)) for part in (inputs, mates)]
    sums = [
        sum(jnp.sum(hidden, 0) for hidden, _ in acts),
        sum(jnp.sum(hidden * hidden, 0) for hidden, _ in acts),
    ]
    (stats,) = exchange([jnp.stack(sums + [sums[0]] * 6)], ("far",), ("gather",), 1)
    stats = jnp.sum(stats[:, :2], 0)
    unit_mean = stats[0] / total_rows
    unit_var = stats[1] / total_rows - unit_mean * unit_mean
    inv_std = lax.rsqrt(unit_var + epsilon)
    centred = [(hidden - unit_mean) * inv_std for hidden, _ in acts]
    normed = [(gain * part + bias).astype(bf16) for part in centred]

    row_share = row_count // mp_count
    partial = jnp.stack([jnp.dot(part, out_rows, preferred_element_type=f32).astype(bf16) for part in normed])
    partial = jnp.where(side == 0, partial, partial[::-1])
    partial = partial.reshape(PAIR * mp_count, row_share, EMB)
    (parts,) = exchange([partial], ("near",), ("scatter",), 2)
    embedding = jnp.sum(parts.astype(f32), 0)

    row_begin = lax.axis_index("mp") * row_share
    dense_part = lax.dynamic_slice_in_dim(dense_vectors, row_begin, row_share, 0)
    label_part = lax.dynamic_slice_in_dim(labels, row_begin, row_share, 0)
    embed_part, loss_local = interact(embedding, dense_part, field_mix, label_part, total_rows)
    grad_embed, losses = exchange(
        [embed_part, jnp.full((8, 128), loss_local, f32)], ("near", "near"), ("gather", "gather"), 3
    )
    loss_part = jnp.sum(losses[:, 0, 0])
    grad_embed = grad_embed.reshape(PAIR, row_count, EMB)
    grad_embed = [grad_embed[side], grad_embed[1 - side]]

    out_local = sum(
        lax.dot_general(part, grad, (((0,), (0,)), ((), ())), preferred_element_type=f32)
        for part, grad in zip(normed, grad_embed)
    )
    grad_normed = [
        lax.dot_general(grad, out_rows, (((1,), (1,)), ((), ())), preferred_element_type=f32)
        for grad in grad_embed
    ]
    sums = [
        sum(jnp.sum(grad, 0) for grad in grad_normed),
        sum(jnp.sum(grad * part, 0) for grad, part in zip(grad_normed, centred)),
        jnp.full((half,), loss_part, f32),
    ]
    stats, out_parts = exchange(
        [jnp.stack(sums + [sums[2]] * 5), out_local.astype(bf16).reshape(far_count, half // far_count, EMB)],
        ("dp", "far"),
        ("gather", "scatter"),
        4,
    )
    stats = jnp.sum(stats.reshape(far_count, PAIR, 8, half), 0)
    grad_bias, grad_gain = stats[:, 0].reshape(-1), stats[:, 1].reshape(-1)
    mean_loss = stats[0, 2, 0] / total_rows
    own_bias, own_gain = stats[side, 0], stats[side, 1]
    out_sum = jnp.sum(out_parts.astype(f32), 0).astype(bf16)

    total = 0.0
    for rows, grad, part, (_, mish_slope) in zip((inputs, mates), grad_normed, centred, acts):
        grad_hidden = inv_std * (
            gain * grad - gain * own_bias / total_rows - part * gain * own_gain / total_rows
        )
        grad_pre = (grad_hidden * mish_slope).astype(bf16)
        total = total + lax.dot_general(
            rows, grad_pre, (((0,), (0,)), ((), ())), preferred_element_type=f32
        )
    blocks = total.astype(bf16).reshape(dp_count, codes // dp_count, half)
    hash_parts, out_blocks = exchange(
        [blocks, out_sum], ("dp", "dp"), ("scatter", "gather"), 5, pl.ANY
    )
    hash_parts = hash_parts.reshape(far_count, PAIR, codes // dp_count, half).astype(f32)
    grad_hash = jnp.concatenate([jnp.sum(hash_parts[:, at], 0) for at in range(PAIR)], 1)
    grad_out = out_blocks.reshape(far_count, PAIR, -1, EMB).swapaxes(0, 1).reshape(units, EMB).astype(f32)
    return (grad_hash, grad_gain, grad_bias, grad_out, mean_loss)


def solution(mesh):
    in_specs = (
        P("dp", None),
        P(None, "mp"),
        P("mp"),
        P("mp"),
        P("mp", None),
        P("dp", None, None),
        P(),
        P("dp"),
    )
    out_specs = (P("dp", "mp"), P("mp"), P("mp"), P("mp", None), P())
    return jax.shard_map(
        on_device, mesh=mesh, in_specs=in_specs, out_specs=out_specs, check_vma=False
    )
```

time: 568 us -> 315 us (0.55)
  waiting for transfers between devices: 389 us -> 0 us
  Pallas kernels: 0 us -> 217 us
  blocking collectives: 74.8 us -> 0 us
  other arithmetic: 5.36 us -> 24.5 us
  matrix products: 76.4 us -> 60.8 us
  between operations: 15.6 us -> 2.74 us
  local copies, waits for them, and re-layouts: 3.08 us -> 9.38 us
    reduce_scatter x2 -> x0, waiting for transfers between devices: 312 us -> none  [the longest x1 283 us: on_device(): lax.psum_scatter(lax.dot_general(inputs, grad_pre, (((0,), (0,)), ((), ()...]
    pallas_call x0 -> x6, Pallas kernels: none -> 217 us  [the longest x5 182 us: exchange(): pl.pallas_call(functools.partial(exchange_kernel, kinds, modes), out_shap...]
    psum x1 -> x0, waiting for transfers between devices: 77.6 us -> none  [on_device(): grad_out, loss_total = lax.psum((out_local, loss_part), 'dp')]
    psum x3 -> x0, blocking collectives: 68 us -> none  [the longest x1 30.6 us: on_device(): lax.psum((jnp.sum(grad_normed, 0), jnp.sum(grad_normed * centred, 0)), 'dp')]
    dot_general x5 -> x10, matrix products: 76.4 us -> 60.8 us  [the longest x2 24.8 us: on_device(): lax.dot_general(rows, grad_pre, (((0,), (0,)), ((), ())), preferred_eleme...]
    convert_element_type x0 -> x3, other arithmetic: none -> 9.27 us  [the longest x1 6.64 us: on_device(): (hash_codes.astype(f32) * (2.0 / (buckets - 1.0)) - 1.0).astype(bf16)]
    all_gather x1 -> x0, blocking collectives: 6.79 us -> none  [on_device(): grad_embed = lax.all_gather(embed_part, 'mp', axis=0, tiled=True)]
    reduce_sum x0 -> x6, other arithmetic: none -> 6.65 us  [the longest x1 1.39 us: on_device(): embedding = jnp.sum(parts.astype(f32), 0)]
  transfers between devices with their start and end apart: 3 -> 0, of which waited for: 3 -> 0; matrix products, arithmetic and copies ran while one was open for 5% -> 0% of each run, Pallas kernels for 0% -> 0%
where the time goes in v1:
time: 315 us; the launch traced here: 314 us
  Pallas kernels  217 us (69%)
  matrix products  60.8 us (19%)
  other arithmetic  24.5 us (8%)
  local copies, waits for them, and re-layouts  9.38 us (3%)
    pallas_call x5, Pallas kernels, exchange(): pl.pallas_call(functools.partial(exchange_kernel, kinds, modes), out_shap...  182 us
    pallas_call x1, Pallas kernels, mate_rows(): pl.pallas_call(functools.partial(share_kernel, pieces), out_shape=jax.Sha...  34.3 us
    dot_general x2, matrix products, on_device(): lax.dot_general(rows, grad_pre, (((0,), (0,)), ((), ())), preferred_eleme...  24.8 us
    dot_general x2, matrix products, on_device(): jnp.dot(part, weights, preferred_element_type=f32)  22.6 us
    convert_element_type x1, other arithmetic, on_device(): (hash_codes.astype(f32) * (2.0 / (buckets - 1.0)) - 1.0).astype(bf16)  6.64 us

profile of v1, /device:TPU:10, one launch (start us, length us, event | category | flops | bytes accessed | tf_op | source)
XLA Modules:
  0.0 314.0 jit_solution(14208096503778396563)
XLA Ops:
  0.6 0.0 copy-start
  0.7 0.8 dynamic_slice.31
  1.5 0.7 dynamic_slice.32
  2.1 6.6 %add_convert_fusion.1.rows_ref = bf16[1024,2048]{1,0:T(8,128)(2,1)} fusion(s32[1024,2048]{1,0:T(8,128)} %param.8), kind=kLoop, calls=%fused_computation.1 | loop fusion | flops 8388608 | bytes 12582912 | tf_op jit(solution)/shard_map/convert_element_type | solution.py:195
  8.8 34.3 %shard_map.119 = bf16[1024,2048]{1,0:T(8,128)(2,1)} custom-call(bf16[1024,2048]{1,0:T(8,128)(2,1)} %add_convert_fusion.1.rows_ref), custom_call_target="tpu_custom_call" | custom-call | tf_op jit(solution)/shard_map/pallas_call | solution.py:168
  43.1 0.0 copy-start.2
  43.1 12.4 %multiply_reduce_fusion.2 = (f32[1024]{0:T(1024)S(1)}, f32[1024]{0:T(1024)S(1)}, f32[1024,1024]{1,0:T(8,128)}, f32[1024,1024]{1,0:T(8,128)}) fusion(bf16[1024,2048]{1,0:T(8,128)(2,1)} %shard_map.119, bf16[2048,2048]{1,0:T(8,128)(2,1)} %param.9, s32[]{:T(128)S(6)} %select_n.38), kind=kOutput, calls=%fused_computation.14 | convolution fusion | flops 4305451008 | bytes 16785412 | tf_op jit(solution)/shard_map/dot_general | solution.py:198
  55.6 0.0 copy-done.2
  55.6 10.1 %multiply_reduce_fusion.3 = (f32[1024]{0:T(1024)S(1)}, f32[1024]{0:T(1024)S(1)}, f32[1024,1024]{1,0:T(8,128)}, f32[1024,1024]{1,0:T(8,128)}) fusion(bf16[1024,2048]{1,0:T(8,128)(2,1)S(1)} %copy-done.2, bf16[2048,2048]{1,0:T(8,128)(2,1)} %param.9, s32[]{:T(128)S(6)} %select_n.38), kind=kOutput, calls=%fused_computation.15 | convolution fusion | flops 4305451008 | bytes 16785412 | tf_op jit(solution)/shard_map/dot_general | solution.py:198
  65.7 0.7 stack.10.refs_0_
  66.4 8.2 %shard_map.120 = f32[4,8,1024]{2,1,0:T(8,128)} custom-call(f32[8,1024]{1,0:T(8,128)} %stack.10.refs_0_), custom_call_target="tpu_custom_call" | custom-call | tf_op jit(solution)/shard_map/pallas_call | solution.py:94
  74.6 0.0 copy-start.6
  74.6 1.1 slice_reduce_fusion.2
  75.7 0.0 copy-done
  75.7 3.2 %fusion.23 = bf16[1,1024,256]{2,1,0:T(8,128)(2,1)S(1)} fusion(bf16[2048,256]{1,0:T(8,128)(2,1)S(1)} %copy-done, s32[]{:T(128)S(6)} %select_n.38, f32[1024,1024]{1,0:T(8,128)} %get-tuple-element.29, f32[1024]{0:T(1024)S(1)} %dynamic_slice.32, f32[1024]{0:T(1024)S(1)} %bitcast.68, f32[1024]{0:T(1024)S(1)} %dynamic_slice.31, f32[1024]{0:T(1024)S(1)} %bitcast.61), kind=kOutput, calls=%fused_computation.52 | convolution fusion | flops 542375936 | bytes 5259268 | tf_op jit(solution)/shard_map/dot_general | solution.py:212
  79.0 0.0 copy-done.6
  79.0 0.8 fusion.22
  79.8 0.0 copy-start.14
  79.8 0.1 pad_maximum_fusion.1
  80.0 1.2 reverse_select_fusion
  81.1 15.6 %shard_map.121 = bf16[8,256,256]{2,1,0:T(8,128)(2,1)} custom-call(bf16[8,256,256]{2,1,0:T(8,128)(2,1)} %bitcast.44), custom_call_target="tpu_custom_call" | custom-call | tf_op jit(solution)/shard_map/pallas_call | solution.py:94
  96.7 1.4 convert_reduce_fusion
  98.1 1.6 fusion.8
  99.7 0.0 copy-done.14
  99.7 0.1 multiply_reduce_fusion.4
  99.8 1.4 fusion.49
  101.2 1.2 broadcast_in_dim.2.refs_1_
  102.4 0.1 multiply_multiply_fusion
  102.5 2.6 fusion.9.refs_0_
  105.1 18.8 %shard_map.122 = (bf16[8,256,256]{2,1,0:T(8,128)(2,1)}, f32[8,8,128]{2,1,0:T(8,128)}) custom-call(bf16[256,256]{1,0:T(8,128)(2,1)} %fusion.9.refs_0_, f32[8,128]{1,0:T(8,128)} %broadcast_in_dim.2.refs_1_), custom_call_target="tpu_custom_call" | custom-call | tf_op jit(solution)/shard_map/pallas_call | solution.py:94
  123.9 1.4 slice_reduce_fusion.3
  125.3 0.6 stack_broadcast_in_dim.2
  126.0 0.0 copy-start.4
  126.0 0.0 copy-start.11
  126.0 3.3 %fusion.27 = f32[1024,256]{1,0:T(8,128)S(1)} fusion(bf16[2,1024,256]{2,1,0:T(8,128)(2,1)} %bitcast.48, s32[]{:T(128)S(6)} %select_n.43, f32[1024,1024]{1,0:T(8,128)} %get-tuple-element.30, f32[1024]{0:T(1024)S(1)} %dynamic_slice.32, f32[1024]{0:T(1024)S(1)} %bitcast.70, f32[1024]{0:T(1024)S(1)} %dynamic_slice.31, f32[1024]{0:T(1024)S(1)} %bitcast.63), kind=kOutput, calls=%fused_computation.57 | convolution fusion | flops 542113792 | bytes 5783556 | tf_op jit(solution)/shard_map/dot_general | solution.py:230
  129.3 0.3 copy-done.4
  129.6 0.3 copy-done.11
  129.9 1.7 fusion.21
  131.6 0.7 fusion.29
  132.3 1.4 copy-done.7
  133.8 3.6 %multiply_reduce_fusion = (f32[1024]{0:T(1024)S(1)}, f32[1024]{0:T(1024)S(1)}, f32[1024]{0:T(1024)S(1)}, f32[1024]{0:T(1024)S(1)}, f32[1024,1024]{1,0:T(8,128)}) fusion(f32[1024,1024]{1,0:T(8,128)S(1)} %copy-done.4, f32[1024]{0:T(1024)S(1)} %bitcast.72, f32[1024]{0:T(1024)S(1)} %bitcast.65, f32[1024,1024]{1,0:T(8,128)S(1)} %fusion.29, ...), kind=kOutput, calls=%fused_computation.8 | convolution fusion | flops 547352576 | bytes 17850376 | tf_op jit(solution)/shard_map/dot_general | solution.py:234
  137.3 0.0 copy-done.3
  137.3 0.7 stack.14.refs_0_
  138.0 23.1 %shard_map.123 = (f32[8,8,1024]{2,1,0:T(8,128)}, bf16[4,256,256]{2,1,0:T(8,128)(2,1)}) custom-call(f32[8,1024]{1,0:T(8,128)} %stack.14.refs_0_, bf16[4,256,256]{2,1,0:T(8,128)(2,1)} %bitcast.52), custom_call_target="tpu_custom_call" | custom-call | tf_op jit(solution)/shard_map/pallas_call | solution.py:94
  161.1 1.0 reduce_sum.189
  162.1 0.5 slice.42
  163.2 0.6 fusion.63
  163.9 0.0 copy-done.13
  163.9 0.0 copy-start.8
  163.9 0.0 copy-start.10
  163.9 0.0 copy-start.15
  163.9 14.7 %fusion.20 = f32[2048,1024]{1,0:T(8,128)} fusion(bf16[1024,2048]{1,0:T(8,128)(2,1)} %add_convert_fusion.1.rows_ref, f32[1024,1024]{1,0:T(8,128)} %get-tuple-element.40, f32[1024,1024]{1,0:T(8,128)} %copy-done.3, f32[1024,1024]{1,0:T(8,128)} %get-tuple-element.30, f32[1024]{0:T(1024)S(1)} %bitcast.81, f32[1024]{0:T(1024)S(1)} %multiply_multiply_fusion.1, ...), kind=kOutput, calls=%fused_computation.45 | convolution fusion | flops 4320133120 | bytes 25186304 | tf_op jit(solution)/shard_map/dot_general | solution.py:260
  178.6 0.0 copy-done.5
  178.6 0.0 copy-done.8
  178.7 10.1 %add_convert_fusion = bf16[2048,1024]{1,0:T(8,128)(2,1)} fusion(f32[2048,1024]{1,0:T(8,128)} %fusion.20, bf16[1024,2048]{1,0:T(8,128)(2,1)S(1)} %copy-done.10, f32[1024,1024]{1,0:T(8,128)S(1)} %copy-done.15, f32[1024,1024]{1,0:T(8,128)S(1)} %copy-done.8, f32[1024,1024]{1,0:T(8,128)S(1)} %copy-done.5, f32[1024]{0:T(1024)S(1)} %bitcast.82, ...), kind=kOutput, calls=%fused_computation | convolution fusion | flops 4324327424 | bytes 29380608 | tf_op jit(solution)/shard_map/dot_general | solution.py:260
  188.7 0.7 reduce_sum.190.refs_1_
  189.5 116.7 %shard_map.124 = (bf16[8,256,1024]{2,1,0:T(8,128)(2,1)}, bf16[8,256,256]{2,1,0:T(8,128)(2,1)}) custom-call(bf16[8,256,1024]{2,1,0:T(8,128)(2,1)} %bitcast.45, bf16[256,256]{1,0:T(8,128)(2,1)} %reduce_sum.190.refs_1_), custom_call_target="tpu_custom_call" | custom-call | tf_op jit(solution)/shard_map/pallas_call | solution.py:94
  306.2 1.6 convert_bitcast_fusion
  307.8 1.5 copy.13
  309.2 0.0 copy-done.9
  309.2 1.1 bitcast_convert_fusion
  310.3 0.0 copy-start.1
  310.3 1.1 slice_reduce_fusion.1
  311.4 1.5 pad_maximum_fusion
  (17 shorter events, 0.1 us)
Async XLA Ops:
  0.6 75.1 %copy-start = (bf16[2048,256]{1,0:T(8,128)(2,1)S(1)}, bf16[2048,256]{1,0:T(8,128)(2,1)}, u32[]{:S(2)}) copy-start(bf16[2048,256]{1,0:T(8,128)(2,1)} %param.12) | copy-start | bytes 3145732
  43.1 12.4 %copy-start.2 = (bf16[1024,2048]{1,0:T(8,128)(2,1)S(1)}, bf16[1024,2048]{1,0:T(8,128)(2,1)}, u32[]{:S(2)}) copy-start(bf16[1024,2048]{1,0:T(8,128)(2,1)} %add_convert_fusion.1.rows_ref) | copy-start | bytes 12582916
  74.6 4.4 %copy-start.6 = (f32[1024,1024]{1,0:T(8,128)S(1)}, f32[1024,1024]{1,0:T(8,128)}, u32[]{:S(2)}) copy-start(f32[1024,1024]{1,0:T(8,128)} %get-tuple-element.30) | copy-start | bytes 12582916
  79.8 19.9 %copy-start.14 = (f32[8]{0:T(128)S(1)}, f32[8]{0:T(128)}, u32[]{:S(2)}) copy-start(f32[8]{0:T(128)} %param.14) | copy-start | bytes 100
  126.0 3.6 %copy-start.4 = (f32[1024,1024]{1,0:T(8,128)S(1)}, f32[1024,1024]{1,0:T(8,128)}, u32[]{:S(2)}) copy-start(f32[1024,1024]{1,0:T(8,128)} %get-tuple-element.29) | copy-start | bytes 12582916
  126.0 3.9 %copy-start.11 = (bf16[8,256,256]{2,1,0:T(8,128)(2,1)S(1)}, bf16[8,256,256]{2,1,0:T(8,128)(2,1)}, u32[]{:S(2)}) copy-start(bf16[8,256,256]{2,1,0:T(8,128)(2,1)} %get-tuple-element.11) | copy-start | bytes 3145732
  131.6 2.2 copy-start.7
  133.8 3.6 %copy-start.3 = (f32[1024,1024]{1,0:T(8,128)}, f32[1024,1024]{1,0:T(8,128)S(1)}, u32[]{:S(2)}) copy-start(f32[1024,1024]{1,0:T(8,128)S(1)} %fusion.29) | copy-start | bytes 12582916
  133.8 30.1 %copy-start.13 = (f32[2048]{0:T(1024)S(1)}, f32[2048]{0:T(1024)}, u32[]{:S(2)}) copy-start(f32[2048]{0:T(1024)} %param.10) | copy-start | bytes 24580
  163.9 14.8 %copy-start.5 = (f32[1024,1024]{1,0:T(8,128)S(1)}, f32[1024,1024]{1,0:T(8,128)}, u32[]{:S(2)}) copy-start(f32[1024,1024]{1,0:T(8,128)} %get-tuple-element.29) | copy-start | bytes 12582916
  163.9 14.8 %copy-start.8 = (f32[1024,1024]{1,0:T(8,128)S(1)}, f32[1024,1024]{1,0:T(8,128)}, u32[]{:S(2)}) copy-start(f32[1024,1024]{1,0:T(8,128)} %get-tuple-element.41) | copy-start | bytes 12582916
  163.9 14.8 %copy-start.10 = (bf16[1024,2048]{1,0:T(8,128)(2,1)S(1)}, bf16[1024,2048]{1,0:T(8,128)(2,1)}, u32[]{:S(2)}) copy-start(bf16[1024,2048]{1,0:T(8,128)(2,1)} %shard_map.119) | copy-start | bytes 12582916
  163.9 14.8 %copy-start.15 = (f32[1024,1024]{1,0:T(8,128)S(1)}, f32[1024,1024]{1,0:T(8,128)}, u32[]{:S(2)}) copy-start(f32[1024,1024]{1,0:T(8,128)} %get-tuple-element.39) | copy-start | bytes 12582916
  178.7 10.1 %copy-start.12 = (bf16[4,256,256]{2,1,0:T(8,128)(2,1)S(1)}, bf16[4,256,256]{2,1,0:T(8,128)(2,1)}, u32[]{:S(2)}) copy-start(bf16[4,256,256]{2,1,0:T(8,128)(2,1)} %get-tuple-element.14) | copy-start | bytes 1572868
  306.2 3.0 copy-start.9
  310.3 2.6 copy-start.1

commit v2 on v1

--- a/solution.py
+++ b/solution.py
@@ -177,6 +177,263 @@
     )(rows)
 
 
+def spread_kernel(count, *refs):
+    sources, results = refs[:count], refs[count : 2 * count]
+    sends, receives, core_sends, core_receives = (
+        refs[(2 + at) * count : (3 + at) * count] for at in range(4)
+    )
+    locals_ = refs[6 * count]
+    dp, mp, mp_n = lax.axis_index("dp"), lax.axis_index("mp"), lax.axis_size("mp")
+    chips = mp_n // 2
+    size = PAIR * chips
+    core = mp % 2
+    here = (dp % PAIR) * chips + mp // 2
+    other = (dp, mp + 1 - 2 * core)
+
+    def device(place):
+        return ((dp // PAIR) * PAIR + place // chips, (place % chips) * 2 + core)
+
+    barrier = pltpu.get_barrier_semaphore()
+    for target in [other] + [device(lax.rem(here + step, size)) for step in range(1, size)]:
+        pl.semaphore_signal(barrier, inc=1, device_id=target, device_id_type=MESH)
+    pl.semaphore_wait(barrier, size)
+    firsts, seconds, owns = [], [], []
+    for at in range(count):
+        slot = here * 2 + core
+        for step in range(1, size):
+            copy = pltpu.make_async_remote_copy(
+                src_ref=sources[at],
+                dst_ref=results[at].at[slot],
+                send_sem=sends[at].at[step - 1],
+                recv_sem=receives[at].at[step - 1],
+                device_id=device(lax.rem(here + step, size)),
+                device_id_type=MESH,
+            )
+            copy.start()
+            firsts.append((at, step, copy))
+        copy = pltpu.make_async_remote_copy(
+            src_ref=sources[at],
+            dst_ref=results[at].at[slot],
+            send_sem=core_sends[at].at[0],
+            recv_sem=core_receives[at].at[0],
+            device_id=other,
+            device_id_type=MESH,
+        )
+        copy.start()
+        seconds.append(copy)
+        copy = pltpu.make_async_copy(sources[at], results[at].at[slot], locals_.at[at])
+        copy.start()
+        owns.append(copy)
+    for at, step, first in firsts:
+        first.wait_recv()
+        slot = lax.rem(here - step + size, size) * 2 + core
+        copy = pltpu.make_async_remote_copy(
+            src_ref=results[at].at[slot],
+            dst_ref=results[at].at[slot],
+            send_sem=core_sends[at].at[step],
+            recv_sem=core_receives[at].at[step],
+            device_id=other,
+            device_id_type=MESH,
+        )
+        copy.start()
+        seconds.append(copy)
+    for copy in seconds + owns:
+        copy.wait()
+    for _, _, first in firsts:
+        first.wait_send()
+
+
+def spread(operands, ident):
+    size = PAIR * (lax.axis_size("mp") // 2)
+    dma = pltpu.SemaphoreType.DMA
+    count = len(operands)
+    return pl.pallas_call(
+        functools.partial(spread_kernel, count),
+        out_shape=[jax.ShapeDtypeStruct((size * 2,) + op.shape, op.dtype) for op in operands],
+        in_specs=[pl.BlockSpec(memory_space=pltpu.VMEM)] * count,
+        out_specs=[pl.BlockSpec(memory_space=pltpu.VMEM)] * count,
+        scratch_shapes=[dma((size - 1,))] * (2 * count) + [dma((size,))] * (2 * count) + [dma((count,))],
+        compiler_params=pltpu.CompilerParams(collective_id=ident, has_side_effects=True),
+    )(*operands)
+
+
+def reduce_kernel(
+    rows, mates, grads, mate_grads, small, out, gathered,
+    total, sending, from_low, from_high, swap_out, swap_in,
+    send_sem, low_sem, high_sem, swap_sem, far_send, far_recv, mate_send, mate_recv, local_sem,
+):
+    dp, mp, dp_n = lax.axis_index("dp"), lax.axis_index("mp"), lax.axis_size("dp")
+    far_n = dp_n // PAIR
+    far, side = dp // PAIR, dp % PAIR
+    mate = (dp + 1 - 2 * side, mp)
+    width, half = swap_out.shape
+
+    barrier = pltpu.get_barrier_semaphore()
+    for step in range(1, dp_n):
+        pl.semaphore_signal(
+            barrier, inc=1, device_id=(lax.rem(dp + step, dp_n), mp), device_id_type=MESH
+        )
+    pl.semaphore_wait(barrier, dp_n - 1)
+
+    def remote(source, target_ref, sent, received, target):
+        return pltpu.make_async_remote_copy(
+            src_ref=source,
+            dst_ref=target_ref,
+            send_sem=sent,
+            recv_sem=received,
+            device_id=target,
+            device_id_type=MESH,
+        )
+
+    def product(block):
+        columns = pl.ds(pl.multiple_of(block * width, width), width)
+        contract = (((0,), (0,)), ((), ()))
+        total[...] = lax.dot_general(
+            rows[:, columns], grads[...], contract, preferred_element_type=jnp.float32
+        ) + lax.dot_general(
+            mates[:, columns], mate_grads[...], contract, preferred_element_type=jnp.float32
+        )
+
+    def upward(to, half_of):
+        return remote(
+            sending.at[to, half_of], from_low.at[to, half_of], send_sem.at[to, half_of],
+            low_sem.at[to, half_of], (lax.rem(dp + PAIR, dp_n), mp),
+        )
+
+    def downward(to, half_of):
+        return remote(
+            sending.at[to, half_of], from_high.at[to, half_of], send_sem.at[to, half_of],
+            high_sem.at[to, half_of], (lax.rem(dp + dp_n - PAIR, dp_n), mp),
+        )
+
+    def add_low(to, half_of):
+        @pl.when(far > 0)
+        def _():
+            upward(to, half_of).wait_recv()
+            total[...] += from_low[to, half_of].astype(jnp.float32)
+
+    def add_high(to, half_of):
+        @pl.when(far < far_n - 1)
+        def _():
+            downward(to, half_of).wait_recv()
+            total[...] += from_high[to, half_of].astype(jnp.float32)
+
+    def place_at(turn):
+        down = (turn // 2) % 2
+        step = turn // 4
+        to = (1 - down) * (far_n - 1 - step) + down * step
+        late = turn % 2
+        half_of = late * side + (1 - late) * (1 - side)
+        return down, to, half_of
+
+    turns = 4 * (far_n - 1)
+
+    def one_turn(turn, carry):
+        down, to, half_of = place_at(turn)
+
+        @pl.when((to - far) * (1 - 2 * down) > 0)
+        def _():
+            product(to * PAIR + half_of)
+
+            @pl.when(down == 0)
+            def _():
+                add_low(to, half_of)
+                sending[to, half_of] = total[...].astype(jnp.bfloat16)
+                upward(to, half_of).start()
+
+            @pl.when(down == 1)
+            def _():
+                add_high(to, half_of)
+                sending[to, half_of] = total[...].astype(jnp.bfloat16)
+                downward(to, half_of).start()
+
+        return carry
+
+    lax.fori_loop(0, turns, one_turn, 0)
+
+    shares = []
+    for step in range(1, far_n):
+        place = lax.rem(far + step, far_n) * PAIR + side
+        shares.append(
+            remote(small, gathered.at[dp], far_send.at[step - 1], far_recv.at[step - 1], (place, mp))
+        )
+    handed = [remote(small, gathered.at[dp], mate_send.at[0], mate_recv.at[0], mate)]
+    own = pltpu.make_async_copy(small, gathered.at[dp], local_sem)
+    for copy in shares + handed + [own]:
+        copy.start()
+
+    swap = remote(swap_out, swap_in, swap_sem.at[0], swap_sem.at[1], mate)
+
+    def last_turn(late, carry):
+        half_of = late * side + (1 - late) * (1 - side)
+        product(far * PAIR + half_of)
+        add_low(far, half_of)
+        add_high(far, half_of)
+
+        @pl.when(late == 0)
+        def _():
+            swap_out[...] = total[...].astype(jnp.bfloat16)
+            swap.start()
+
+        @pl.when(late == 1)
+        def _():
+            out[:, pl.ds(pl.multiple_of(side * half, half), half)] = total[...]
+
+        return carry
+
+    lax.fori_loop(0, 2, last_turn, 0)
+
+    for step in range(1, far_n):
+        shares[step - 1].wait_recv()
+        slot = lax.rem(far - step + far_n, far_n) * PAIR + side
+        copy = remote(gathered.at[slot], gathered.at[slot], mate_send.at[step], mate_recv.at[step], mate)
+        copy.start()
+        handed.append(copy)
+    swap.wait_recv()
+    out[:, pl.ds(pl.multiple_of((1 - side) * half, half), half)] = swap_in[...].astype(jnp.float32)
+    swap.wait_send()
+
+    def sent_turn(turn, carry):
+        down, to, half_of = place_at(turn)
+
+        @pl.when((to - far) * (1 - 2 * down) > 0)
+        def _():
+            upward(to, half_of).wait_send()
+
+        return carry
+
+    lax.fori_loop(0, turns, sent_turn, 0)
+    for copy in shares:
+        copy.wait_send()
+    for copy in handed:
+        copy.wait()
+    own.wait()
+
+
+def reduce_codes(rows, mates, grads, mate_grads, small, ident):
+    dp_n = lax.axis_size("dp")
+    far_n = dp_n // PAIR
+    width, half = rows.shape[1] // dp_n, grads.shape[1]
+    bf16, dma = jnp.bfloat16, pltpu.SemaphoreType.DMA
+    vmem = pl.BlockSpec(memory_space=pltpu.VMEM)
+    buffer = pltpu.VMEM((far_n, PAIR, width, half), bf16)
+    return pl.pallas_call(
+        reduce_kernel,
+        out_shape=[
+            jax.ShapeDtypeStruct((width, PAIR * half), jnp.float32),
+            jax.ShapeDtypeStruct((dp_n,) + small.shape, small.dtype),
+        ],
+        in_specs=[vmem] * 5,
+        out_specs=[vmem] * 2,
+        scratch_shapes=[pltpu.VMEM((width, half), jnp.float32)]
+        + [buffer] * 3
+        + [pltpu.VMEM((width, half), bf16)] * 2
+        + [dma((far_n, PAIR))] * 3
+        + [dma((2,)), dma((far_n - 1,)), dma((far_n - 1,)), dma((far_n,)), dma((far_n,)), dma(())],
+        compiler_params=pltpu.CompilerParams(collective_id=ident, has_side_effects=True),
+    )(rows, mates, grads, mate_grads, small)
+
+
 def on_device(hash_codes, w_hash, norm_gain, norm_bias, w_out, dense_vectors, field_mix, labels):
     row_count = hash_codes.shape[0]
     dp_count = lax.axis_size("dp")
@@ -219,9 +476,7 @@
     dense_part = lax.dynamic_slice_in_dim(dense_vectors, row_begin, row_share, 0)
     label_part = lax.dynamic_slice_in_dim(labels, row_begin, row_share, 0)
     embed_part, loss_local = interact(embedding, dense_part, field_mix, label_part, total_rows)
-    grad_embed, losses = exchange(
-        [embed_part, jnp.full((8, 128), loss_local, f32)], ("near", "near"), ("gather", "gather"), 3
-    )
+    grad_embed, losses = spread([embed_part, jnp.full((8, 128), loss_local, f32)], 3)
     loss_part = jnp.sum(losses[:, 0, 0])
     grad_embed = grad_embed.reshape(PAIR, row_count, EMB)
     grad_embed = [grad_embed[side], grad_embed[1 - side]]
@@ -251,21 +506,13 @@
     own_bias, own_gain = stats[side, 0], stats[side, 1]
     out_sum = jnp.sum(out_parts.astype(f32), 0).astype(bf16)
 
-    total = 0.0
-    for rows, grad, part, (_, mish_slope) in zip((inputs, mates), grad_normed, centred, acts):
+    grad_pres = []
+    for grad, part, (_, mish_slope) in zip(grad_normed, centred, acts):
         grad_hidden = inv_std * (
             gain * grad - gain * own_bias / total_rows - part * gain * own_gain / total_rows
         )
-        grad_pre = (grad_hidden * mish_slope).astype(bf16)
-        total = total + lax.dot_general(
-            rows, grad_pre, (((0,), (0,)), ((), ())), preferred_element_type=f32
-        )
-    blocks = total.astype(bf16).reshape(dp_count, codes // dp_count, half)
-    hash_parts, out_blocks = exchange(
-        [blocks, out_sum], ("dp", "dp"), ("scatter", "gather"), 5, pl.ANY
-    )
-    hash_parts = hash_parts.reshape(far_count, PAIR, codes // dp_count, half).astype(f32)
-    grad_hash = jnp.concatenate([jnp.sum(hash_parts[:, at], 0) for at in range(PAIR)], 1)
+        grad_pres.append((grad_hidden * mish_slope).astype(bf16))
+    grad_hash, out_blocks = reduce_codes(inputs, mates, *grad_pres, out_sum, 5)
     grad_out = out_blocks.reshape(far_count, PAIR, -1, EMB).swapaxes(0, 1).reshape(units, EMB).astype(f32)
     return (grad_hash, grad_gain, grad_bias, grad_out, mean_loss)
 

time: 315 us -> 289 us (0.917)
  matrix products: 60.8 us -> 36 us
  Pallas kernels: 217 us -> 202 us
  other arithmetic: 24.5 us -> 34.6 us
    pallas_call x5 -> x3, Pallas kernels: 182 us -> 47.3 us  [exchange(): pl.pallas_call(functools.partial(exchange_kernel, kinds, modes), out_shap...]
    pallas_call x0 -> x2, Pallas kernels: none -> 120 us  [the longest x1 107 us: reduce_codes(): pl.pallas_call(reduce_kernel, out_shape=[jax.ShapeDtypeStruct((width, PAI...]
    dot_general x2 -> x0, matrix products: 24.8 us -> none  [on_device(): lax.dot_general(rows, grad_pre, (((0,), (0,)), ((), ())), preferred_eleme...]
    convert_element_type x1, other arithmetic: 1.07 us -> 13.8 us  [on_device(): grad_pres.append((grad_hidden * mish_slope).astype(bf16))]
where the time goes in v2:
time: 289 us; the launch traced here: 286 us
  Pallas kernels  202 us (70%)
  matrix products  36 us (12%)
  other arithmetic  34.6 us (12%)
  local copies, waits for them, and re-layouts  10.7 us (4%)
    pallas_call x1, Pallas kernels, reduce_codes(): pl.pallas_call(reduce_kernel, out_shape=[jax.ShapeDtypeStruct((width, PAI...  107 us
    pallas_call x3, Pallas kernels, exchange(): pl.pallas_call(functools.partial(exchange_kernel, kinds, modes), out_shap...  47.3 us
    pallas_call x1, Pallas kernels, mate_rows(): pl.pallas_call(functools.partial(share_kernel, pieces), out_shape=jax.Sha...  34.3 us
    dot_general x2, matrix products, on_device(): jnp.dot(part, weights, preferred_element_type=f32)  22.7 us
    convert_element_type x1, other arithmetic, on_device(): grad_pres.append((grad_hidden * mish_slope).astype(bf16))  13.8 us
    pallas_call x1, Pallas kernels, spread(): pl.pallas_call(functools.partial(spread_kernel, count), out_shape=[jax.Sh...  13.3 us
    convert_element_type x1, other arithmetic, on_device(): (hash_codes.astype(f32) * (2.0 / (buckets - 1.0)) - 1.0).astype(bf16)  6.6 us

profile of v2, /device:TPU:10, one launch (start us, length us, event | category | flops | bytes accessed | tf_op | source)
XLA Modules:
  0.0 285.9 jit_solution(14053291350857106667)
XLA Ops:
  0.6 0.0 copy-start
  0.7 0.8 dynamic_slice.31
  1.4 0.7 dynamic_slice.32
  2.1 6.6 %add_convert_fusion.rows_ref.rows = bf16[1024,2048]{1,0:T(8,128)(2,1)} fusion(s32[1024,2048]{1,0:T(8,128)} %param.8), kind=kLoop, calls=%fused_computation | loop fusion | flops 8388608 | bytes 12582912 | tf_op jit(solution)/shard_map/convert_element_type | solution.py:452
  8.7 34.3 %shard_map.119.mates = bf16[1024,2048]{1,0:T(8,128)(2,1)} custom-call(bf16[1024,2048]{1,0:T(8,128)(2,1)} %add_convert_fusion.rows_ref.rows), custom_call_target="tpu_custom_call" | custom-call | tf_op jit(solution)/shard_map/pallas_call | solution.py:168
  43.1 0.0 copy-start.1
  43.1 12.5 %multiply_reduce_fusion.2 = (f32[1024]{0:T(1024)S(1)}, f32[1024]{0:T(1024)S(1)}, f32[1024,1024]{1,0:T(8,128)}, f32[1024,1024]{1,0:T(8,128)}) fusion(bf16[1024,2048]{1,0:T(8,128)(2,1)} %shard_map.119.mates, bf16[2048,2048]{1,0:T(8,128)(2,1)} %param.9, s32[]{:T(128)S(6)} %select_n.38), kind=kOutput, calls=%fused_computation.11 | convolution fusion | flops 4305451008 | bytes 16785412 | tf_op jit(solution)/shard_map/dot_general | solution.py:455
  55.6 0.0 copy-done.1
  55.6 10.1 %multiply_reduce_fusion.3 = (f32[1024]{0:T(1024)S(1)}, f32[1024]{0:T(1024)S(1)}, f32[1024,1024]{1,0:T(8,128)}, f32[1024,1024]{1,0:T(8,128)}) fusion(bf16[1024,2048]{1,0:T(8,128)(2,1)S(1)} %copy-done.1, bf16[2048,2048]{1,0:T(8,128)(2,1)} %param.9, s32[]{:T(128)S(6)} %select_n.38), kind=kOutput, calls=%fused_computation.12 | convolution fusion | flops 4305451008 | bytes 16785412 | tf_op jit(solution)/shard_map/dot_general | solution.py:455
  65.8 0.7 stack.10.refs_0_
  66.4 8.3 %shard_map.120 = f32[4,8,1024]{2,1,0:T(8,128)} custom-call(f32[8,1024]{1,0:T(8,128)} %stack.10.refs_0_), custom_call_target="tpu_custom_call" | custom-call | tf_op jit(solution)/shard_map/pallas_call | solution.py:94
  74.7 0.0 copy-start.4
  74.7 1.1 slice_reduce_fusion
  75.8 0.0 copy-done
  75.8 3.2 %fusion.12 = bf16[1,1024,256]{2,1,0:T(8,128)(2,1)S(1)} fusion(bf16[2048,256]{1,0:T(8,128)(2,1)S(1)} %copy-done, s32[]{:T(128)S(6)} %select_n.38, f32[1024,1024]{1,0:T(8,128)} %get-tuple-element.27, f32[1024]{0:T(1024)S(1)} %dynamic_slice.32, f32[1024]{0:T(1024)S(1)} %bitcast.60, f32[1024]{0:T(1024)S(1)} %dynamic_slice.31, f32[1024]{0:T(1024)S(1)} %bitcast.54), kind=kOutput, calls=%fused_computation.37 | convolution fusion | flops 542375936 | bytes 5259268 | tf_op jit(solution)/shard_map/dot_general | solution.py:469
  79.0 0.0 copy-done.4
  79.0 0.9 fusion.11
  79.9 0.0 copy-start.10
  79.9 0.1 pad_maximum_fusion
  80.0 1.2 reverse_select_fusion
  81.2 15.6 %shard_map.121 = bf16[8,256,256]{2,1,0:T(8,128)(2,1)} custom-call(bf16[8,256,256]{2,1,0:T(8,128)(2,1)} %bitcast.38), custom_call_target="tpu_custom_call" | custom-call | tf_op jit(solution)/shard_map/pallas_call | solution.py:94
  96.8 1.4 convert_reduce_fusion
  98.2 1.6 fusion.8
  99.8 0.0 copy-done.10
  99.9 0.1 multiply_reduce_fusion.4
  100.0 1.4 fusion.38
  101.3 1.2 broadcast_in_dim.2.refs_1_
  102.6 0.1 multiply_multiply_fusion
  102.7 2.6 fusion.9.refs_0_
  105.3 13.3 %shard_map.122 = (bf16[8,256,256]{2,1,0:T(8,128)(2,1)}, f32[8,8,128]{2,1,0:T(8,128)}) custom-call(bf16[256,256]{1,0:T(8,128)(2,1)} %fusion.9.refs_0_, f32[8,128]{1,0:T(8,128)} %broadcast_in_dim.2.refs_1_), custom_call_target="tpu_custom_call" | custom-call | tf_op jit(solution)/shard_map/pallas_call | solution.py:250
  118.6 1.4 slice_reduce_fusion.1
  119.9 0.6 stack_broadcast_in_dim.2
  120.6 0.0 copy-start.3
  120.6 0.0 copy-start.7
  120.6 3.3 %fusion.16 = f32[1024,256]{1,0:T(8,128)S(1)} fusion(bf16[2,1024,256]{2,1,0:T(8,128)(2,1)} %bitcast.41, s32[]{:T(128)S(6)} %select_n.43, f32[1024,1024]{1,0:T(8,128)} %get-tuple-element.28, f32[1024]{0:T(1024)S(1)} %dynamic_slice.32, f32[1024]{0:T(1024)S(1)} %bitcast.62, f32[1024]{0:T(1024)S(1)} %dynamic_slice.31, f32[1024]{0:T(1024)S(1)} %bitcast.56), kind=kOutput, calls=%fused_computation.42 | convolution fusion | flops 542113792 | bytes 5783556 | tf_op jit(solution)/shard_map/dot_general | solution.py:485
  123.9 0.3 copy-done.3
  124.2 0.3 copy-done.7
  124.5 1.7 fusion.10
  126.2 0.0 copy-start.5
  126.2 0.7 fusion.18
  127.0 1.4 copy-done.5
  128.4 0.0 copy-start.2
  128.4 0.0 copy-start.9
  128.4 3.5 %multiply_reduce_fusion = (f32[1024]{0:T(1024)S(1)}, f32[1024]{0:T(1024)S(1)}, f32[1024]{0:T(1024)S(1)}, f32[1024]{0:T(1024)S(1)}, f32[1024,1024]{1,0:T(8,128)}) fusion(f32[1024,1024]{1,0:T(8,128)S(1)} %copy-done.3, f32[1024]{0:T(1024)S(1)} %bitcast.64, f32[1024]{0:T(1024)S(1)} %bitcast.58, f32[1024,1024]{1,0:T(8,128)S(1)} %fusion.18, ...), kind=kOutput, calls=%fused_computation.5 | convolution fusion | flops 547352576 | bytes 17850376 | tf_op jit(solution)/shard_map/dot_general | solution.py:489
  131.9 0.0 copy-done.2
  131.9 0.7 stack.14.refs_0_
  132.6 23.4 %shard_map.123 = (f32[8,8,1024]{2,1,0:T(8,128)}, bf16[4,256,256]{2,1,0:T(8,128)(2,1)}) custom-call(f32[8,1024]{1,0:T(8,128)} %stack.14.refs_0_, bf16[4,256,256]{2,1,0:T(8,128)(2,1)} %bitcast.45), custom_call_target="tpu_custom_call" | custom-call | tf_op jit(solution)/shard_map/pallas_call | solution.py:94
  156.0 1.0 reduce_sum.171
  157.0 0.5 slice.32
  158.2 0.6 fusion.42
  158.8 0.0 copy-done.9
  158.8 0.0 copy-start.8
  158.8 13.8 %multiply_convert_fusion = (bf16[1024,1024]{1,0:T(8,128)(2,1)}, bf16[1024,1024]{1,0:T(8,128)(2,1)}) fusion(f32[1024,1024]{1,0:T(8,128)} %get-tuple-element.39, f32[1024,1024]{1,0:T(8,128)} %get-tuple-element.41, f32[1024,1024]{1,0:T(8,128)} %get-tuple-element.27, f32[1024]{0:T(1024)S(1)} %bitcast.66, f32[1024]{0:T(1024)S(1)} %multiply_multiply_fusion.1, ...), kind=kLoop, calls=%fused_computation.3 | loop fusion | flops 50331648 | bytes 29380608 | tf_op jit(solution)/shard_map/convert_element_type | solution.py:514
  172.6 0.0 copy-done.8
  172.6 0.7 reduce_sum.172.small
  173.3 107.0 %shard_map.124 = (f32[256,2048]{1,0:T(8,128)}, bf16[8,256,256]{2,1,0:T(8,128)(2,1)}) custom-call(bf16[1024,2048]{1,0:T(8,128)(2,1)} %add_convert_fusion.rows_ref.rows, bf16[1024,2048]{1,0:T(8,128)(2,1)} %shard_map.119.mates, bf16[1024,1024]{1,0:T(8,128)(2,1)} %get-tuple-element.34.grads, bf16[1024,1024]{1,0:T(8,128)(2,1)} %get-tuple-element.33.mate_grads, ...), custom_call_target="tpu_custom_call" | custom-call | tf_op jit(solution)/shard_map/pallas_call | solution.py:420
  280.4 0.0 copy-start.6
  280.4 1.6 convert_bitcast_fusion
  281.9 1.5 copy.13
  283.4 0.0 copy-done.6
  283.4 1.3 copy.15
  (7 shorter events, 0.1 us)
Async XLA Ops:
  0.6 75.2 %copy-start = (bf16[2048,256]{1,0:T(8,128)(2,1)S(1)}, bf16[2048,256]{1,0:T(8,128)(2,1)}, u32[]{:S(2)}) copy-start(bf16[2048,256]{1,0:T(8,128)(2,1)} %param.12) | copy-start | bytes 3145732
  43.1 12.5 %copy-start.1 = (bf16[1024,2048]{1,0:T(8,128)(2,1)S(1)}, bf16[1024,2048]{1,0:T(8,128)(2,1)}, u32[]{:S(2)}) copy-start(bf16[1024,2048]{1,0:T(8,128)(2,1)} %add_convert_fusion.rows_ref.rows) | copy-start | bytes 12582916
  74.7 4.3 %copy-start.4 = (f32[1024,1024]{1,0:T(8,128)S(1)}, f32[1024,1024]{1,0:T(8,128)}, u32[]{:S(2)}) copy-start(f32[1024,1024]{1,0:T(8,128)} %get-tuple-element.28) | copy-start | bytes 12582916
  79.9 19.9 %copy-start.10 = (f32[8]{0:T(128)S(1)}, f32[8]{0:T(128)}, u32[]{:S(2)}) copy-start(f32[8]{0:T(128)} %param.14) | copy-start | bytes 100
  120.6 3.6 %copy-start.3 = (f32[1024,1024]{1,0:T(8,128)S(1)}, f32[1024,1024]{1,0:T(8,128)}, u32[]{:S(2)}) copy-start(f32[1024,1024]{1,0:T(8,128)} %get-tuple-element.27) | copy-start | bytes 12582916
  120.6 3.9 %copy-start.7 = (bf16[8,256,256]{2,1,0:T(8,128)(2,1)S(1)}, bf16[8,256,256]{2,1,0:T(8,128)(2,1)}, u32[]{:S(2)}) copy-start(bf16[8,256,256]{2,1,0:T(8,128)(2,1)} %get-tuple-element.11) | copy-start | bytes 3145732
  126.2 2.2 copy-start.5
  128.4 3.5 %copy-start.2 = (f32[1024,1024]{1,0:T(8,128)}, f32[1024,1024]{1,0:T(8,128)S(1)}, u32[]{:S(2)}) copy-start(f32[1024,1024]{1,0:T(8,128)S(1)} %fusion.18) | copy-start | bytes 12582916
  128.4 30.4 %copy-start.9 = (f32[2048]{0:T(1024)S(1)}, f32[2048]{0:T(1024)}, u32[]{:S(2)}) copy-start(f32[2048]{0:T(1024)} %param.10) | copy-start | bytes 24580
  158.8 13.8 %copy-start.8 = (bf16[4,256,256]{2,1,0:T(8,128)(2,1)S(1)}, bf16[4,256,256]{2,1,0:T(8,128)(2,1)}, u32[]{:S(2)}) copy-start(bf16[4,256,256]{2,1,0:T(8,128)(2,1)} %get-tuple-element.14) | copy-start | bytes 1572868
  280.4 3.0 %copy-start.6 = (f32[256,2048]{1,0:T(8,128)S(1)}, f32[256,2048]{1,0:T(8,128)}, u32[]{:S(2)}) copy-start(f32[256,2048]{1,0:T(8,128)} %get-tuple-element.47) | copy-start | bytes 6291460

commit v3 on v2

--- a/solution.py
+++ b/solution.py
@@ -101,13 +101,25 @@
     )(*operands)
 
 
-def share_kernel(pieces, rows_ref, out_ref, near_send, near_recv, far_send, far_recv, core_send, core_recv):
+def share_kernel(
+    pieces, rows_ref, weights_ref, out_ref, hidden_ref, slope_ref, sums_ref,
+    rows_here, weights_here, near_send, near_recv, far_send, far_recv, core_send, core_recv, load_sem,
+):
     dp, mp, mp_n = lax.axis_index("dp"), lax.axis_index("mp"), lax.axis_size("mp")
     chips = mp_n // 2
     chip, core = mp // 2, mp % 2
     mate = (dp + 1 - 2 * (dp % PAIR), mp)
     other = (dp, mp + 1 - 2 * core)
     length = rows_ref.shape[0] // (mp_n * pieces)
+    depth = rows_ref.shape[0] // pieces
+    half = weights_here.shape[1]
+    mine = pl.ds(pl.multiple_of((dp % PAIR) * half, half), half)
+    loads = [
+        pltpu.make_async_copy(weights_ref.at[:, mine], weights_here, load_sem.at[0]),
+        pltpu.make_async_copy(rows_ref, rows_here, load_sem.at[1]),
+    ]
+    for load in loads:
+        load.start()
 
     def across(step):
         return (dp, lax.rem(chip + step, chips) * 2 + core)
@@ -127,6 +139,15 @@
         copy.start()
         return copy
 
+    def activate(piece):
+        chunk = pl.ds(pl.multiple_of(piece * depth, depth), depth)
+        pre_act = jnp.dot(rows_here[chunk, :], weights_here[...], preferred_element_type=jnp.float32)
+        hidden, slope = mish_parts(pre_act)
+        hidden_ref[chunk, :] = hidden
+        slope_ref[chunk, :] = slope.astype(slope_ref.dtype)
+        sums_ref[0:1, :] += jnp.sum(hidden, 0, keepdims=True)
+        sums_ref[1:2, :] += jnp.sum(hidden * hidden, 0, keepdims=True)
+
     barrier = pltpu.get_barrier_semaphore()
     for target in [mate, other] + [across(step) for step in range(1, chips)]:
         pl.semaphore_signal(barrier, inc=1, device_id=target, device_id_type=MESH)
@@ -136,8 +157,12 @@
         send(rows_ref, mp, piece, near_send.at[piece], near_recv.at[piece], mate)
         for piece in range(pieces)
     ]
+    sums_ref[...] = jnp.zeros_like(sums_ref)
+    for load in loads:
+        load.wait()
     far, cores = [], []
     for piece in range(pieces):
+        lax.fori_loop(piece, piece + 1, lambda at, carry: (activate(at), carry)[1], 0)
         near[piece].wait_recv()
         far.append(
             [
@@ -161,20 +186,30 @@
             copy.wait_send()
 
 
-def mate_rows(rows, ident):
+def mate_rows(rows, weights, ident):
     chips = lax.axis_size("mp") // 2
     pieces = 4
     dma = pltpu.SemaphoreType.DMA
+    row_count, codes = rows.shape
+    half = weights.shape[1] // PAIR
+    anywhere, vmem = pl.BlockSpec(memory_space=pl.ANY), pl.BlockSpec(memory_space=pltpu.VMEM)
     return pl.pallas_call(
         functools.partial(share_kernel, pieces),
-        out_shape=jax.ShapeDtypeStruct(rows.shape, rows.dtype),
-        in_specs=[pl.BlockSpec(memory_space=pl.ANY)],
-        out_specs=pl.BlockSpec(memory_space=pl.ANY),
-        scratch_shapes=[dma((pieces,)), dma((pieces,))]
+        out_shape=[
+            jax.ShapeDtypeStruct(rows.shape, rows.dtype),
+            jax.ShapeDtypeStruct((row_count, half), jnp.float32),
+            jax.ShapeDtypeStruct((row_count, half), jnp.bfloat16),
+            jax.ShapeDtypeStruct((8, half), jnp.float32),
+        ],
+        in_specs=[anywhere, anywhere],
+        out_specs=[anywhere, vmem, vmem, vmem],
+        scratch_shapes=[pltpu.VMEM(rows.shape, rows.dtype), pltpu.VMEM((codes, half), weights.dtype)]
+        + [dma((pieces,)), dma((pieces,))]
         + [dma((pieces, max(chips - 1, 1)))] * 2
-        + [dma((pieces, chips))] * 2,
+        + [dma((pieces, chips))] * 2
+        + [dma((2,))],
         compiler_params=pltpu.CompilerParams(collective_id=ident, has_side_effects=True),
-    )(rows)
+    )(rows, weights)
 
 
 def spread_kernel(count, *refs):
@@ -450,13 +485,11 @@
 
     weights, gain, bias, out_rows = mine(w_hash, 1), mine(norm_gain, 0), mine(norm_bias, 0), mine(w_out, 0)
     inputs = (hash_codes.astype(f32) * (2.0 / (buckets - 1.0)) - 1.0).astype(bf16)
-    mates = mate_rows(inputs, 0)
-
-    acts = [mish_parts(jnp.dot(part, weights, preferred_element_type=f32)) for part in (inputs, mates)]
-    sums = [
-        sum(jnp.sum(hidden, 0) for hidden, _ in acts),
-        sum(jnp.sum(hidden * hidden, 0) for hidden, _ in acts),
-    ]
+    mates, own_hidden, own_slope, own_sums = mate_rows(inputs, w_hash, 0)
+
+    hidden, mish_slope = mish_parts(jnp.dot(mates, weights, preferred_element_type=f32))
+    acts = [(own_hidden, own_slope), (hidden, mish_slope.astype(bf16))]
+    sums = [own_sums[0] + jnp.sum(hidden, 0), own_sums[1] + jnp.sum(hidden * hidden, 0)]
     (stats,) = exchange([jnp.stack(sums + [sums[0]] * 6)], ("far",), ("gather",), 1)
     stats = jnp.sum(stats[:, :2], 0)
     unit_mean = stats[0] / total_rows
@@ -506,6 +539,11 @@
     own_bias, own_gain = stats[side, 0], stats[side, 1]
     out_sum = jnp.sum(out_parts.astype(f32), 0).astype(bf16)
 
+    grad_embed = lax.optimization_barrier(grad_embed)
+    grad_normed = [
+        lax.dot_general(grad, out_rows, (((1,), (1,)), ((), ())), preferred_element_type=f32)
+        for grad in grad_embed
+    ]
     grad_pres = []
     for grad, part, (_, mish_slope) in zip(grad_normed, centred, acts):
         grad_hidden = inv_std * (

time: 289 us -> 278 us (0.962)
  other arithmetic: 34.6 us -> 21.6 us
  Pallas kernels: 202 us -> 205 us
    convert_element_type x1 -> x0, other arithmetic: 13.8 us -> none  [on_device(): grad_pres.append((grad_hidden * mish_slope).astype(bf16))]
    dot_general x2 -> x4, matrix products: 4.24 us -> 15.3 us  [on_device(): lax.dot_general(grad, out_rows, (((1,), (1,)), ((), ())), preferred_eleme...]
    dot_general x2 -> x1, matrix products: 22.7 us -> 12.3 us  [on_device(): jnp.dot(mates, weights, preferred_element_type=f32)]
where the time goes in v3:
time: 278 us; the launch traced here: 275 us
  Pallas kernels  205 us (74%)
  matrix products  36.6 us (13%)
  other arithmetic  21.6 us (8%)
  local copies, waits for them, and re-layouts  9.22 us (3%)
    pallas_call x1, Pallas kernels, reduce_codes(): pl.pallas_call(reduce_kernel, out_shape=[jax.ShapeDtypeStruct((width, PAI...  107 us
    pallas_call x3, Pallas kernels, exchange(): pl.pallas_call(functools.partial(exchange_kernel, kinds, modes), out_shap...  47.2 us
    pallas_call x1, Pallas kernels, mate_rows(): pl.pallas_call(functools.partial(share_kernel, pieces), out_shape=[jax.Sh...  37.1 us
    dot_general x4, matrix products, on_device(): lax.dot_general(grad, out_rows, (((1,), (1,)), ((), ())), preferred_eleme...  15.3 us
    pallas_call x1, Pallas kernels, spread(): pl.pallas_call(functools.partial(spread_kernel, count), out_shape=[jax.Sh...  13.2 us
    dot_general x1, matrix products, on_device(): jnp.dot(mates, weights, preferred_element_type=f32)  12.3 us
    convert_element_type x1, other arithmetic, on_device(): (hash_codes.astype(f32) * (2.0 / (buckets - 1.0)) - 1.0).astype(bf16)  6.69 us

profile of v3, /device:TPU:10, one launch (start us, length us, event | category | flops | bytes accessed | tf_op | source)
XLA Modules:
  0.0 274.7 jit_solution(10802495885988143473)
XLA Ops:
  0.6 0.0 copy-start
  0.6 6.7 %add_convert_fusion.rows_ref.rows = bf16[1024,2048]{1,0:T(8,128)(2,1)} fusion(s32[1024,2048]{1,0:T(8,128)} %param.8), kind=kLoop, calls=%fused_computation | loop fusion | flops 8388608 | bytes 12582912 | tf_op jit(solution)/shard_map/convert_element_type | solution.py:487
  7.3 37.1 %shard_map.119 = (bf16[1024,2048]{1,0:T(8,128)(2,1)}, f32[1024,1024]{1,0:T(8,128)}, bf16[1024,1024]{1,0:T(8,128)(2,1)}, f32[8,1024]{1,0:T(8,128)}) custom-call(bf16[1024,2048]{1,0:T(8,128)(2,1)} %add_convert_fusion.rows_ref.rows, bf16[2048,2048]{1,0:T(8,128)(2,1)} %weights_ref.1), custom_call_target="tpu_custom_call" | custom-call | tf_op jit(solution)/shard_map/pallas_call | solution.py:196
  44.4 0.0 copy-start.9
  44.4 0.0 copy-start.7
  44.5 12.3 %multiply_reduce_fusion.2 = (f32[1024]{0:T(1024)S(1)}, f32[1024]{0:T(1024)S(1)}, f32[1024,1024]{1,0:T(8,128)}, f32[1024,1024]{1,0:T(8,128)}) fusion(bf16[1024,2048]{1,0:T(8,128)(2,1)} %get-tuple-element.17.mates, bf16[2048,2048]{1,0:T(8,128)(2,1)} %weights_ref.1, s32[]{:T(128)S(6)} %select_n.38), kind=kOutput, calls=%fused_computation.11 | convolution fusion | flops 4305451008 | bytes 16785412 | tf_op jit(solution)/shard_map/dot_general | solution.py:490
  56.8 0.0 copy-done.9
  56.8 0.8 slice_add_fusion
  57.6 0.7 stack.10.refs_0_
  58.3 8.2 %shard_map.120 = f32[4,8,1024]{2,1,0:T(8,128)} custom-call(f32[8,1024]{1,0:T(8,128)} %stack.10.refs_0_), custom_call_target="tpu_custom_call" | custom-call | tf_op jit(solution)/shard_map/pallas_call | solution.py:94
  66.5 0.0 copy-start.1
  66.6 1.1 slice_reduce_fusion
  67.7 0.0 copy-done.7
  67.7 0.0 copy-done
  67.7 3.2 %fusion.8 = bf16[1,1024,256]{2,1,0:T(8,128)(2,1)S(1)} fusion(bf16[2048,256]{1,0:T(8,128)(2,1)S(1)} %copy-done, s32[]{:T(128)S(6)} %select_n.38, f32[1024,1024]{1,0:T(8,128)} %get-tuple-element.37, f32[1024]{0:T(1024)S(1)} %dynamic_slice.32, f32[1024]{0:T(1024)S(1)} %bitcast.48, f32[1024]{0:T(1024)S(1)} %dynamic_slice.31, f32[1024]{0:T(1024)S(1)} %bitcast.41), kind=kOutput, calls=%fused_computation.30 | convolution fusion | flops 542375936 | bytes 5259268 | tf_op jit(solution)/shard_map/dot_general | solution.py:502
  70.9 0.0 copy-done.1
  70.9 0.8 fusion.7
  71.7 0.0 copy-start.8
  71.8 0.1 pad_maximum_fusion
  71.9 1.2 reverse_select_fusion
  73.0 15.6 %shard_map.121 = bf16[8,256,256]{2,1,0:T(8,128)(2,1)} custom-call(bf16[8,256,256]{2,1,0:T(8,128)(2,1)} %bitcast.35), custom_call_target="tpu_custom_call" | custom-call | tf_op jit(solution)/shard_map/pallas_call | solution.py:94
  88.6 1.4 convert_reduce_fusion
  90.0 1.6 fusion.4
  91.6 0.0 copy-done.8
  91.6 0.1 multiply_reduce_fusion.3
  91.7 1.4 fusion.27
  93.1 0.1 multiply_multiply_fusion
  93.2 2.6 fusion.5.refs_0_
  95.8 1.2 broadcast_in_dim.2.refs_1_
  97.0 13.2 %shard_map.122 = (bf16[8,256,256]{2,1,0:T(8,128)(2,1)}, f32[8,8,128]{2,1,0:T(8,128)}) custom-call(bf16[256,256]{1,0:T(8,128)(2,1)} %fusion.5.refs_0_, f32[8,128]{1,0:T(8,128)} %broadcast_in_dim.2.refs_1_), custom_call_target="tpu_custom_call" | custom-call | tf_op jit(solution)/shard_map/pallas_call | solution.py:285
  110.3 0.0 copy-start.2
  110.3 1.4 dynamic-slice_bitcast_fusion
  111.7 0.7 fusion.12
  112.5 0.3 copy-done.2
  112.8 3.7 %multiply_reduce_fusion = (f32[1024]{0:T(1024)S(1)}, f32[1024]{0:T(1024)S(1)}, f32[1024]{0:T(1024)S(1)}, f32[1024]{0:T(1024)S(1)}) fusion(f32[1024,1024]{1,0:T(8,128)} %get-tuple-element.37, f32[1024]{0:T(1024)S(1)} %bitcast.50, f32[1024]{0:T(1024)S(1)} %bitcast.43, f32[1024,1024]{1,0:T(8,128)S(1)} %fusion.12, f32[1024,1024]{1,0:T(8,128)S(1)} %copy-done.2, ...), kind=kOutput, calls=%fused_computation.5 | convolution fusion | flops 547352576 | bytes 13656068 | tf_op jit(solution)/shard_map/dot_general | solution.py:522
  116.5 1.4 slice_reduce_fusion.1
  117.9 0.6 stack_broadcast_in_dim.2
  118.6 0.7 stack.14.refs_0_
  119.2 0.0 copy-start.3
  119.2 3.2 %fusion.17 = f32[1024,256]{1,0:T(8,128)S(1)} fusion(bf16[1024,256]{1,0:T(8,128)(2,1)S(1)} %get-tuple-element.21, f32[1024,1024]{1,0:T(8,128)} %get-tuple-element.19, f32[1024]{0:T(1024)S(1)} %dynamic_slice.32, f32[1024]{0:T(1024)S(1)} %bitcast.51, f32[1024]{0:T(1024)S(1)} %dynamic_slice.31, f32[1024]{0:T(1024)S(1)} %bitcast.44), kind=kOutput, calls=%fused_computation.44 | convolution fusion | flops 542113792 | bytes 5783552 | tf_op jit(solution)/shard_map/dot_general | solution.py:518
  122.4 0.3 copy-done.3
  122.7 1.7 fusion.6
  124.4 23.4 %shard_map.123 = (f32[8,8,1024]{2,1,0:T(8,128)}, bf16[4,256,256]{2,1,0:T(8,128)(2,1)}) custom-call(f32[8,1024]{1,0:T(8,128)} %stack.14.refs_0_, bf16[4,256,256]{2,1,0:T(8,128)(2,1)} %bitcast.39), custom_call_target="tpu_custom_call" | custom-call | tf_op jit(solution)/shard_map/pallas_call | solution.py:94
  147.8 1.0 reduce_sum.157
  148.9 0.0 copy-start.4
  148.9 0.0 copy-start.10
  148.9 6.0 %multiply_convert_fusion.1.grads = bf16[1024,1024]{1,0:T(8,128)(2,1)} fusion(bf16[1024,1024]{1,0:T(8,128)(2,1)} %get-tuple-element.24, f32[1024,1024]{1,0:T(8,128)} %get-tuple-element.19, bf16[1024,256]{1,0:T(8,128)(2,1)S(1)} %get-tuple-element.21, f32[1024]{0:T(1024)S(1)} %bitcast.60, f32[1024]{0:T(1024)S(1)} %multiply_multiply_fusion.1, ...), kind=kOutput, calls=%fused_computation.4 | convolution fusion | flops 549453824 | bytes 9457668 | tf_op jit(solution)/shard_map/dot_general | solution.py:544
  154.9 0.0 copy-done.4
  154.9 0.0 copy-done.10
  154.9 0.0 copy-start.6
  154.9 4.8 %multiply_convert_fusion.mate_grads = bf16[1024,1024]{1,0:T(8,128)(2,1)} fusion(f32[1024,1024]{1,0:T(8,128)S(1)} %copy-done.4, bf16[1024,256]{1,0:T(8,128)(2,1)S(1)} %get-tuple-element.25, f32[1024,1024]{1,0:T(8,128)S(1)} %copy-done.10, f32[1024]{0:T(1024)S(1)} %bitcast.61, f32[1024]{0:T(1024)S(1)} %multiply_multiply_fusion.1, f32[1024]{0:T(1024)S(1)} %bitcast.54, ...), kind=kOutput, calls=%fused_computation.2 | convolution fusion | flops 564133888 | bytes 11554820 | tf_op jit(solution)/shard_map/dot_general | solution.py:544
  159.7 0.0 copy-done.6
  159.7 0.7 reduce_sum.158.small
  160.5 107.0 %shard_map.124 = (f32[256,2048]{1,0:T(8,128)}, bf16[8,256,256]{2,1,0:T(8,128)(2,1)}) custom-call(bf16[1024,2048]{1,0:T(8,128)(2,1)} %add_convert_fusion.rows_ref.rows, bf16[1024,2048]{1,0:T(8,128)(2,1)} %get-tuple-element.17.mates, bf16[1024,1024]{1,0:T(8,128)(2,1)} %multiply_convert_fusion.1.grads, bf16[1024,1024]{1,0:T(8,128)(2,1)} %multiply_convert_fusion.mate_grads, ...), custom_call_target="tpu_custom_call" | custom-call | tf_op jit(solution)/shard_map/pallas_call | solution.py:455
  267.5 0.0 copy-start.5
  267.5 0.6 fusion.30
  268.1 1.4 convert_bitcast_fusion
  269.6 1.5 copy.13
  271.0 0.5 slice.40
  272.2 0.0 copy-done.5
  272.2 1.3 copy.15
  (7 shorter events, 0.1 us)
Async XLA Ops:
  0.6 67.1 %copy-start = (bf16[2048,256]{1,0:T(8,128)(2,1)S(1)}, bf16[2048,256]{1,0:T(8,128)(2,1)}, u32[]{:S(2)}) copy-start(bf16[2048,256]{1,0:T(8,128)(2,1)} %param.12) | copy-start | bytes 3145732
  44.4 12.3 %copy-start.9 = (f32[2048]{0:T(1024)S(1)}, f32[2048]{0:T(1024)}, u32[]{:S(2)}) copy-start(f32[2048]{0:T(1024)} %param.11) | copy-start | bytes 24580
  44.4 23.2 %copy-start.7 = (f32[2048]{0:T(1024)S(1)}, f32[2048]{0:T(1024)}, u32[]{:S(2)}) copy-start(f32[2048]{0:T(1024)} %param.10) | copy-start | bytes 24580
  66.5 4.3 %copy-start.1 = (f32[1024,1024]{1,0:T(8,128)S(1)}, f32[1024,1024]{1,0:T(8,128)}, u32[]{:S(2)}) copy-start(f32[1024,1024]{1,0:T(8,128)} %get-tuple-element.19) | copy-start | bytes 12582916
  71.7 19.9 %copy-start.8 = (f32[8]{0:T(128)S(1)}, f32[8]{0:T(128)}, u32[]{:S(2)}) copy-start(f32[8]{0:T(128)} %param.14) | copy-start | bytes 100
  110.3 2.5 copy-start.2
  119.2 3.4 %copy-start.3 = (f32[1024,1024]{1,0:T(8,128)S(1)}, f32[1024,1024]{1,0:T(8,128)}, u32[]{:S(2)}) copy-start(f32[1024,1024]{1,0:T(8,128)} %get-tuple-element.37) | copy-start | bytes 12582916
  148.9 6.1 %copy-start.4 = (f32[1024,1024]{1,0:T(8,128)S(1)}, f32[1024,1024]{1,0:T(8,128)}, u32[]{:S(2)}) copy-start(f32[1024,1024]{1,0:T(8,128)} %get-tuple-element.37) | copy-start | bytes 12582916
  148.9 6.1 %copy-start.10 = (f32[1024,1024]{1,0:T(8,128)S(1)}, f32[1024,1024]{1,0:T(8,128)}, u32[]{:S(2)}) copy-start(f32[1024,1024]{1,0:T(8,128)} %get-tuple-element.50) | copy-start | bytes 12582916
  154.9 4.8 %copy-start.6 = (bf16[4,256,256]{2,1,0:T(8,128)(2,1)S(1)}, bf16[4,256,256]{2,1,0:T(8,128)(2,1)}, u32[]{:S(2)}) copy-start(bf16[4,256,256]{2,1,0:T(8,128)(2,1)} %get-tuple-element.26) | copy-start | bytes 1572868
  267.5 4.7 %copy-start.5 = (f32[256,2048]{1,0:T(8,128)S(1)}, f32[256,2048]{1,0:T(8,128)}, u32[]{:S(2)}) copy-start(f32[256,2048]{1,0:T(8,128)} %get-tuple-element.56) | copy-start | bytes 6291460

commit v4 on v3

--- a/solution.py
+++ b/solution.py
@@ -353,6 +353,17 @@
             downward(to, half_of).wait_recv()
             total[...] += from_high[to, half_of].astype(jnp.float32)
 
+    shares = []
+    for step in range(1, far_n):
+        place = lax.rem(far + step, far_n) * PAIR + side
+        shares.append(
+            remote(small, gathered.at[dp], far_send.at[step - 1], far_recv.at[step - 1], (place, mp))
+        )
+    handed = [remote(small, gathered.at[dp], mate_send.at[0], mate_recv.at[0], mate)]
+    own = pltpu.make_async_copy(small, gathered.at[dp], local_sem)
+    for copy in shares + handed + [own]:
+        copy.start()
+
     def place_at(turn):
         down = (turn // 2) % 2
         step = turn // 4
@@ -385,17 +396,6 @@
         return carry
 
     lax.fori_loop(0, turns, one_turn, 0)
-
-    shares = []
-    for step in range(1, far_n):
-        place = lax.rem(far + step, far_n) * PAIR + side
-        shares.append(
-            remote(small, gathered.at[dp], far_send.at[step - 1], far_recv.at[step - 1], (place, mp))
-        )
-    handed = [remote(small, gathered.at[dp], mate_send.at[0], mate_recv.at[0], mate)]
-    own = pltpu.make_async_copy(small, gathered.at[dp], local_sem)
-    for copy in shares + handed + [own]:
-        copy.start()
 
     swap = remote(swap_out, swap_in, swap_sem.at[0], swap_sem.at[1], mate)
 

time: 278 us -> 277 us (level)
  no operation moved by 1% of the time
where the time goes in v4:
time: 277 us; the launch traced here: 276 us
  Pallas kernels  206 us (74%)
  matrix products  36.6 us (13%)
  other arithmetic  21.6 us (8%)
  local copies, waits for them, and re-layouts  9.22 us (3%)
    pallas_call x1, Pallas kernels, reduce_codes(): pl.pallas_call(reduce_kernel, out_shape=[jax.ShapeDtypeStruct((width, PAI...  108 us
    pallas_call x3, Pallas kernels, exchange(): pl.pallas_call(functools.partial(exchange_kernel, kinds, modes), out_shap...  47.2 us
    pallas_call x1, Pallas kernels, mate_rows(): pl.pallas_call(functools.partial(share_kernel, pieces), out_shape=[jax.Sh...  37.1 us
    dot_general x4, matrix products, on_device(): lax.dot_general(grad, out_rows, (((1,), (1,)), ((), ())), preferred_eleme...  15.3 us
    pallas_call x1, Pallas kernels, spread(): pl.pallas_call(functools.partial(spread_kernel, count), out_shape=[jax.Sh...  13.2 us
    dot_general x1, matrix products, on_device(): jnp.dot(mates, weights, preferred_element_type=f32)  12.3 us
    convert_element_type x1, other arithmetic, on_device(): (hash_codes.astype(f32) * (2.0 / (buckets - 1.0)) - 1.0).astype(bf16)  6.69 us

profile of v4, /device:TPU:10, one launch (start us, length us, event | category | flops | bytes accessed | tf_op | source)
XLA Modules:
  0.0 276.0 jit_solution(10271581326920183285)
XLA Ops:
  0.6 0.0 copy-start
  0.6 6.7 %add_convert_fusion.rows_ref.rows = bf16[1024,2048]{1,0:T(8,128)(2,1)} fusion(s32[1024,2048]{1,0:T(8,128)} %param.8), kind=kLoop, calls=%fused_computation | loop fusion | flops 8388608 | bytes 12582912 | tf_op jit(solution)/shard_map/convert_element_type | solution.py:487
  7.3 37.1 %shard_map.119 = (bf16[1024,2048]{1,0:T(8,128)(2,1)}, f32[1024,1024]{1,0:T(8,128)}, bf16[1024,1024]{1,0:T(8,128)(2,1)}, f32[8,1024]{1,0:T(8,128)}) custom-call(bf16[1024,2048]{1,0:T(8,128)(2,1)} %add_convert_fusion.rows_ref.rows, bf16[2048,2048]{1,0:T(8,128)(2,1)} %weights_ref.1), custom_call_target="tpu_custom_call" | custom-call | tf_op jit(solution)/shard_map/pallas_call | solution.py:196
  44.4 0.0 copy-start.9
  44.4 0.0 copy-start.7
  44.5 12.3 %multiply_reduce_fusion.2 = (f32[1024]{0:T(1024)S(1)}, f32[1024]{0:T(1024)S(1)}, f32[1024,1024]{1,0:T(8,128)}, f32[1024,1024]{1,0:T(8,128)}) fusion(bf16[1024,2048]{1,0:T(8,128)(2,1)} %get-tuple-element.17.mates, bf16[2048,2048]{1,0:T(8,128)(2,1)} %weights_ref.1, s32[]{:T(128)S(6)} %select_n.38), kind=kOutput, calls=%fused_computation.11 | convolution fusion | flops 4305451008 | bytes 16785412 | tf_op jit(solution)/shard_map/dot_general | solution.py:490
  56.8 0.0 copy-done.9
  56.8 0.8 slice_add_fusion
  57.6 0.7 stack.10.refs_0_
  58.3 8.2 %shard_map.120 = f32[4,8,1024]{2,1,0:T(8,128)} custom-call(f32[8,1024]{1,0:T(8,128)} %stack.10.refs_0_), custom_call_target="tpu_custom_call" | custom-call | tf_op jit(solution)/shard_map/pallas_call | solution.py:94
  66.5 0.0 copy-start.1
  66.6 1.1 slice_reduce_fusion
  67.7 0.0 copy-done.7
  67.7 0.0 copy-done
  67.7 3.2 %fusion.8 = bf16[1,1024,256]{2,1,0:T(8,128)(2,1)S(1)} fusion(bf16[2048,256]{1,0:T(8,128)(2,1)S(1)} %copy-done, s32[]{:T(128)S(6)} %select_n.38, f32[1024,1024]{1,0:T(8,128)} %get-tuple-element.37, f32[1024]{0:T(1024)S(1)} %dynamic_slice.32, f32[1024]{0:T(1024)S(1)} %bitcast.48, f32[1024]{0:T(1024)S(1)} %dynamic_slice.31, f32[1024]{0:T(1024)S(1)} %bitcast.41), kind=kOutput, calls=%fused_computation.30 | convolution fusion | flops 542375936 | bytes 5259268 | tf_op jit(solution)/shard_map/dot_general | solution.py:502
  70.9 0.0 copy-done.1
  70.9 0.8 fusion.7
  71.7 0.0 copy-start.8
  71.8 0.1 pad_maximum_fusion
  71.9 1.2 reverse_select_fusion
  73.0 15.6 %shard_map.121 = bf16[8,256,256]{2,1,0:T(8,128)(2,1)} custom-call(bf16[8,256,256]{2,1,0:T(8,128)(2,1)} %bitcast.35), custom_call_target="tpu_custom_call" | custom-call | tf_op jit(solution)/shard_map/pallas_call | solution.py:94
  88.6 1.4 convert_reduce_fusion
  90.0 1.6 fusion.4
  91.6 0.0 copy-done.8
  91.6 0.1 multiply_reduce_fusion.3
  91.7 1.4 fusion.27
  93.1 0.1 multiply_multiply_fusion
  93.2 2.6 fusion.5.refs_0_
  95.8 1.2 broadcast_in_dim.2.refs_1_
  97.0 13.2 %shard_map.122 = (bf16[8,256,256]{2,1,0:T(8,128)(2,1)}, f32[8,8,128]{2,1,0:T(8,128)}) custom-call(bf16[256,256]{1,0:T(8,128)(2,1)} %fusion.5.refs_0_, f32[8,128]{1,0:T(8,128)} %broadcast_in_dim.2.refs_1_), custom_call_target="tpu_custom_call" | custom-call | tf_op jit(solution)/shard_map/pallas_call | solution.py:285
  110.3 0.0 copy-start.2
  110.3 1.4 dynamic-slice_bitcast_fusion
  111.7 0.7 fusion.12
  112.5 0.3 copy-done.2
  112.8 3.7 %multiply_reduce_fusion = (f32[1024]{0:T(1024)S(1)}, f32[1024]{0:T(1024)S(1)}, f32[1024]{0:T(1024)S(1)}, f32[1024]{0:T(1024)S(1)}) fusion(f32[1024,1024]{1,0:T(8,128)} %get-tuple-element.37, f32[1024]{0:T(1024)S(1)} %bitcast.50, f32[1024]{0:T(1024)S(1)} %bitcast.43, f32[1024,1024]{1,0:T(8,128)S(1)} %fusion.12, f32[1024,1024]{1,0:T(8,128)S(1)} %copy-done.2, ...), kind=kOutput, calls=%fused_computation.5 | convolution fusion | flops 547352576 | bytes 13656068 | tf_op jit(solution)/shard_map/dot_general | solution.py:522
  116.5 1.4 slice_reduce_fusion.1
  117.9 0.6 stack_broadcast_in_dim.2
  118.6 0.7 stack.14.refs_0_
  119.2 0.0 copy-start.3
  119.2 3.2 %fusion.17 = f32[1024,256]{1,0:T(8,128)S(1)} fusion(bf16[1024,256]{1,0:T(8,128)(2,1)S(1)} %get-tuple-element.21, f32[1024,1024]{1,0:T(8,128)} %get-tuple-element.19, f32[1024]{0:T(1024)S(1)} %dynamic_slice.32, f32[1024]{0:T(1024)S(1)} %bitcast.51, f32[1024]{0:T(1024)S(1)} %dynamic_slice.31, f32[1024]{0:T(1024)S(1)} %bitcast.44), kind=kOutput, calls=%fused_computation.44 | convolution fusion | flops 542113792 | bytes 5783552 | tf_op jit(solution)/shard_map/dot_general | solution.py:518
  122.4 0.3 copy-done.3
  122.7 1.7 fusion.6
  124.4 23.4 %shard_map.123 = (f32[8,8,1024]{2,1,0:T(8,128)}, bf16[4,256,256]{2,1,0:T(8,128)(2,1)}) custom-call(f32[8,1024]{1,0:T(8,128)} %stack.14.refs_0_, bf16[4,256,256]{2,1,0:T(8,128)(2,1)} %bitcast.39), custom_call_target="tpu_custom_call" | custom-call | tf_op jit(solution)/shard_map/pallas_call | solution.py:94
  147.8 1.0 reduce_sum.157
  148.9 0.0 copy-start.4
  148.9 0.0 copy-start.10
  148.9 6.0 %multiply_convert_fusion.1.grads = bf16[1024,1024]{1,0:T(8,128)(2,1)} fusion(bf16[1024,1024]{1,0:T(8,128)(2,1)} %get-tuple-element.24, f32[1024,1024]{1,0:T(8,128)} %get-tuple-element.19, bf16[1024,256]{1,0:T(8,128)(2,1)S(1)} %get-tuple-element.21, f32[1024]{0:T(1024)S(1)} %bitcast.60, f32[1024]{0:T(1024)S(1)} %multiply_multiply_fusion.1, ...), kind=kOutput, calls=%fused_computation.4 | convolution fusion | flops 549453824 | bytes 9457668 | tf_op jit(solution)/shard_map/dot_general | solution.py:544
  154.9 0.0 copy-done.4
  154.9 0.0 copy-done.10
  154.9 0.0 copy-start.6
  154.9 4.8 %multiply_convert_fusion.mate_grads = bf16[1024,1024]{1,0:T(8,128)(2,1)} fusion(f32[1024,1024]{1,0:T(8,128)S(1)} %copy-done.4, bf16[1024,256]{1,0:T(8,128)(2,1)S(1)} %get-tuple-element.25, f32[1024,1024]{1,0:T(8,128)S(1)} %copy-done.10, f32[1024]{0:T(1024)S(1)} %bitcast.61, f32[1024]{0:T(1024)S(1)} %multiply_multiply_fusion.1, f32[1024]{0:T(1024)S(1)} %bitcast.54, ...), kind=kOutput, calls=%fused_computation.2 | convolution fusion | flops 564133888 | bytes 11554820 | tf_op jit(solution)/shard_map/dot_general | solution.py:544
  159.7 0.0 copy-done.6
  159.7 0.7 reduce_sum.158.small
  160.5 108.4 %shard_map.124 = (f32[256,2048]{1,0:T(8,128)}, bf16[8,256,256]{2,1,0:T(8,128)(2,1)}) custom-call(bf16[1024,2048]{1,0:T(8,128)(2,1)} %add_convert_fusion.rows_ref.rows, bf16[1024,2048]{1,0:T(8,128)(2,1)} %get-tuple-element.17.mates, bf16[1024,1024]{1,0:T(8,128)(2,1)} %multiply_convert_fusion.1.grads, bf16[1024,1024]{1,0:T(8,128)(2,1)} %multiply_convert_fusion.mate_grads, ...), custom_call_target="tpu_custom_call" | custom-call | tf_op jit(solution)/shard_map/pallas_call | solution.py:455
  268.9 0.0 copy-start.5
  268.9 0.6 fusion.30
  269.5 1.4 convert_bitcast_fusion
  271.0 1.5 copy.13
  272.4 0.5 slice.40
  273.6 0.0 copy-done.5
  273.6 1.3 copy.15
  (7 shorter events, 0.1 us)
Async XLA Ops:
  0.6 67.1 %copy-start = (bf16[2048,256]{1,0:T(8,128)(2,1)S(1)}, bf16[2048,256]{1,0:T(8,128)(2,1)}, u32[]{:S(2)}) copy-start(bf16[2048,256]{1,0:T(8,128)(2,1)} %param.12) | copy-start | bytes 3145732
  44.4 12.3 %copy-start.9 = (f32[2048]{0:T(1024)S(1)}, f32[2048]{0:T(1024)}, u32[]{:S(2)}) copy-start(f32[2048]{0:T(1024)} %param.11) | copy-start | bytes 24580
  44.4 23.2 %copy-start.7 = (f32[2048]{0:T(1024)S(1)}, f32[2048]{0:T(1024)}, u32[]{:S(2)}) copy-start(f32[2048]{0:T(1024)} %param.10) | copy-start | bytes 24580
  66.5 4.3 %copy-start.1 = (f32[1024,1024]{1,0:T(8,128)S(1)}, f32[1024,1024]{1,0:T(8,128)}, u32[]{:S(2)}) copy-start(f32[1024,1024]{1,0:T(8,128)} %get-tuple-element.19) | copy-start | bytes 12582916
  71.7 19.9 %copy-start.8 = (f32[8]{0:T(128)S(1)}, f32[8]{0:T(128)}, u32[]{:S(2)}) copy-start(f32[8]{0:T(128)} %param.14) | copy-start | bytes 100
  110.3 2.5 copy-start.2
  119.2 3.4 %copy-start.3 = (f32[1024,1024]{1,0:T(8,128)S(1)}, f32[1024,1024]{1,0:T(8,128)}, u32[]{:S(2)}) copy-start(f32[1024,1024]{1,0:T(8,128)} %get-tuple-element.37) | copy-start | bytes 12582916
  148.9 6.1 %copy-start.4 = (f32[1024,1024]{1,0:T(8,128)S(1)}, f32[1024,1024]{1,0:T(8,128)}, u32[]{:S(2)}) copy-start(f32[1024,1024]{1,0:T(8,128)} %get-tuple-element.37) | copy-start | bytes 12582916
  148.9 6.1 %copy-start.10 = (f32[1024,1024]{1,0:T(8,128)S(1)}, f32[1024,1024]{1,0:T(8,128)}, u32[]{:S(2)}) copy-start(f32[1024,1024]{1,0:T(8,128)} %get-tuple-element.50) | copy-start | bytes 12582916
  154.9 4.8 %copy-start.6 = (bf16[4,256,256]{2,1,0:T(8,128)(2,1)S(1)}, bf16[4,256,256]{2,1,0:T(8,128)(2,1)}, u32[]{:S(2)}) copy-start(bf16[4,256,256]{2,1,0:T(8,128)(2,1)} %get-tuple-element.26) | copy-start | bytes 1572868
  268.9 4.7 %copy-start.5 = (f32[256,2048]{1,0:T(8,128)S(1)}, f32[256,2048]{1,0:T(8,128)}, u32[]{:S(2)}) copy-start(f32[256,2048]{1,0:T(8,128)} %get-tuple-element.56) | copy-start | bytes 6291460
